TPU v7x, 256 devices: a whole 4x4x8 slice. The times are simulated.
256 devices in a mesh: chan: 128 (over y, x, z_lo, core), cyl: 2 (over z_hi).
Axes of the slice: x: 4, y: 4, z: 8 (z_hi: 2, z_lo: 4; z = z_hi * 4 + z_lo), core: 2. Of those that a mesh axis runs over, the one named last changes fastest.
Arguments:
- volts: bfloat16 [1024, 4, 2, 64, 512], P('chan', 'cyl'), may hold values from -6 to 6
- gain_exponents: int32 [1024, 4], P('chan', 'cyl'), may hold values from -1 to 1
Outputs:
- intensity: float32 [4, 256, 2, 16384], P('cyl', 'chan')
All inputs are finite; a program needn't handle non-finite values.
Results may differ from a plain program's by a relative error of at most 0.0042.
Values may be sent and summed in bfloat16 or wider, within the bound.
No kernel may reach another device: no remote copies, remote signals or barrier semaphores. Data moves between devices by JAX's collectives and lax.ppermute only.
A program may use at most 128 MiB of HBM per device.

v0:
```python
import math

import jax
import jax.numpy as jnp
import ml_dtypes
import numpy as np
from jax import lax
from jax.experimental import pallas as pl
from jax.experimental.pallas import tpu as pltpu
from jax.sharding import PartitionSpec as P

CYLS = 4
UP = 16
FRAMES = 2
POLS = 2
SUMS = 2
FEEDS = 256
LANES = 128


def ns_rows(feeds):
    feed = np.arange(feeds)
    beam = np.arange(feeds).reshape(feeds // 2, 2).T.reshape(-1)
    theta = (feed[None, :] * (beam[:, None] - feeds // 2) % feeds) * (2.0 * math.pi / feeds)
    cosine = np.cos(theta) / math.sqrt(feeds)
    sine = np.sin(theta) / math.sqrt(feeds)
    real = np.concatenate([cosine, sine], axis=1)
    imag = np.concatenate([-sine, cosine], axis=1)
    return np.concatenate([real, imag], axis=0).astype(np.float32).astype(ml_dtypes.bfloat16)


def up_columns(up, chans):
    index = np.arange(up)
    theta = (index[:, None] * index[None, :] % up) * (2.0 * math.pi / up)
    cosine = np.cos(theta) / math.sqrt(up)
    sine = np.sin(theta) / math.sqrt(up)
    eye = np.eye(chans)
    table = [[np.kron(eye, cosine), np.kron(eye, -sine)], [np.kron(eye, sine), np.kron(eye, cosine)]]
    return np.block(table).astype(np.float32).astype(ml_dtypes.bfloat16)


def rounded(value):
    return value.astype(jnp.bfloat16).astype(jnp.float32)


def ew_beams(real, imag):
    s = math.sqrt(0.5) / 2.0
    h0r, h0i = real[0] * 0.5, imag[0] * 0.5
    n1r, n1i = real[1] * s, imag[1] * s
    a1, b1 = n1r + n1i, n1r - n1i
    h2r, h2i = real[2] * 0.5, imag[2] * 0.5
    n3r, n3i = real[3] * s, imag[3] * s
    a3, b3 = n3r + n3i, n3r - n3i
    first = [
        (h0r - a1, h0i + b1),
        (h0r + b1, h0i + a1),
        (h0r + a1, h0i - b1),
        (h0r - b1, h0i - a1),
    ]
    second = [
        (h2i + b3, a3 - h2r),
        (-h2i - a3, h2r + b3),
        (h2i - b3, -h2r - a3),
        (a3 - h2i, h2r - b3),
    ]
    return [
        (
            (rounded(f[0]) + rounded(g[0])).astype(jnp.bfloat16),
            (rounded(f[1]) + rounded(g[1])).astype(jnp.bfloat16),
        )
        for f, g in zip(first, second)
    ]


def step_kernel(first, last, *refs):
    refs = list(refs)
    k_ref, own_ref, recv_ref, t_ref, u_ref = refs[:5]
    refs = refs[5:]
    acc_in = None if first else refs.pop(0)
    scale_ref = refs.pop(0) if last else None
    out_ref = refs.pop(0)
    x_ref = refs.pop(0)
    stage_ref = refs.pop(0) if last else None
    k = k_ref[0]
    for cyl in range(2):
        mine = pl.ds(pl.multiple_of((2 * k + cyl) * LANES, LANES), LANES)
        other = pl.ds(pl.multiple_of((2 * (1 - k) + cyl) * LANES, LANES), LANES)
        x_ref[mine, :] = own_ref[:, cyl, 0].reshape(LANES, 2 * FEEDS)
        x_ref[other, :] = recv_ref[:, cyl].reshape(LANES, 2 * FEEDS)
    dims = (((1,), (1,)), ((), ()))
    half = FEEDS // 2
    for low in range(2):
        x = x_ref[...]
        rows = pl.ds(low * half, half)
        real = lax.dot_general(t_ref[rows, :], x, dims, preferred_element_type=jnp.float32)
        rows_i = pl.ds(FEEDS + low * half, half)
        imag = lax.dot_general(t_ref[rows_i, :], x, dims, preferred_element_type=jnp.float32)
        cut = lambda v: [v[:, c * LANES : (c + 1) * LANES] for c in range(CYLS)]
        coded = ew_beams(cut(real), cut(imag))
        for e in range(CYLS):
            both = jnp.concatenate(coded[e], axis=1)
            spectra = jnp.dot(both, u_ref[...], preferred_element_type=jnp.float32)
            squared = spectra * spectra
            power = squared[:, :LANES] + squared[:, LANES:]
            if not first:
                power = acc_in[e, rows, :] + power
            if last:
                stage_ref[pl.ds(2 * e + low, half, stride=8), :] = power * scale_ref[pl.ds(e, 1), :]
            else:
                out_ref[e, rows, :] = power
    if last:
        out_ref[...] = stage_ref[...].astype(jnp.bfloat16)


def step(pol, block, first, last, k, volts, recv, table, up_table, acc, scale):
    chans, cyls = volts.shape[:2]
    whole = lambda a: pl.BlockSpec(a.shape, lambda i, kk: (0,) * a.ndim)
    args = [volts, recv, table, up_table]
    specs = [
        pl.BlockSpec(
            (chans, cyls, 1, UP, 2 * FEEDS), lambda i, kk: (0, 0, pol, SUMS * kk[0] + block, 0)
        ),
        whole(recv),
        whole(table),
        whole(up_table),
    ]
    aliases = {}
    if not first:
        aliases = {} if last else {len(args) + 1: 0}
        args.append(acc)
        specs.append(whole(acc))
    if last:
        args.append(scale)
        specs.append(whole(scale))
        out = jax.ShapeDtypeStruct((FEEDS * CYLS, LANES), jnp.bfloat16)
    else:
        out = jax.ShapeDtypeStruct((CYLS, FEEDS, LANES), jnp.float32)
    scratch = [pltpu.VMEM((CYLS * LANES, 2 * FEEDS), jnp.bfloat16)]
    if last:
        scratch.append(pltpu.VMEM((FEEDS * CYLS, LANES), jnp.float32))
    flops = 2 * 512 * 512 * 512 + 2 * CYLS * 256 * 256 * 256
    return pl.pallas_call(
        lambda *refs: step_kernel(first, last, *refs),
        out_shape=out,
        grid_spec=pltpu.PrefetchScalarGridSpec(
            num_scalar_prefetch=1,
            grid=(1,),
            in_specs=specs,
            out_specs=whole(out),
            scratch_shapes=scratch,
        ),
        input_output_aliases=aliases,
        cost_estimate=pl.CostEstimate(flops=flops, bytes_accessed=2 << 20, transcendentals=0),
        compiler_params=pltpu.CompilerParams(vmem_limit_bytes=24 << 20),
        name="beam_step_last" if last else "beam_step",
    )(k, *args)


def place_kernel(in_ref, out_ref, wide_ref):
    wide_ref[...] = in_ref[...].astype(jnp.float32)
    for row in range(4):
        out_ref[row] = wide_ref[pl.ds(row, 256, stride=4), :]


def place(arrived):
    return pl.pallas_call(
        place_kernel,
        out_shape=jax.ShapeDtypeStruct((4, 256, LANES), jnp.float32),
        scratch_shapes=[pltpu.VMEM((1024, LANES), jnp.float32)],
        compiler_params=pltpu.CompilerParams(vmem_limit_bytes=24 << 20),
        name="place",
    )(arrived)


def local(volts, gain_exponents):
    chans, cyls = volts.shape[:2]
    k = lax.axis_index("cyl")
    pair = [(0, 1), (1, 0)]
    table = jnp.asarray(ns_rows(FEEDS))
    up_table = jnp.asarray(up_columns(UP, chans))
    steps = [(pol, block) for pol in range(POLS) for block in range(SUMS)]
    received = []
    source = volts
    for pol, block in steps:
        start = (1 - k) * (SUMS * UP) + block * UP
        piece = lax.dynamic_slice(source, (0, 0, pol, start, 0), (chans, cyls, 1, UP, 2 * FEEDS))
        source, piece = lax.optimization_barrier((source, piece))
        received.append(lax.ppermute(piece.reshape(chans, cyls, UP, 2 * FEEDS), "cyl", pair))
    others = lax.ppermute(gain_exponents, "cyl", pair)
    low = jnp.where(k == 0, gain_exponents, others)
    high = jnp.where(k == 0, others, gain_exponents)
    gains = jnp.exp2(2.0 * jnp.concatenate([low, high], axis=1).astype(jnp.float32)) / (POLS * SUMS)
    scale = jnp.repeat(gains.T, UP, axis=1)
    which = k.astype(jnp.int32).reshape(1)
    acc = None
    for index, (pol, block) in enumerate(steps):
        first, last = index == 0, index == len(steps) - 1
        acc = step(pol, block, first, last, which, volts, received[index], table, up_table, acc, scale)
    sent = acc.reshape(256, 4, LANES)
    arrived = lax.all_to_all(sent, ("chan", "cyl"), split_axis=0, concat_axis=0, tiled=True)
    placed = place(arrived.reshape(1024, LANES))
    placed = placed.reshape(2, 2, 128, FRAMES, LANES).transpose(0, 1, 3, 2, 4)
    return placed.reshape(2, 2, FRAMES, 128 * LANES)


def solution(mesh):
    return jax.shard_map(
        local,
        mesh=mesh,
        in_specs=(P("chan", "cyl", None, None, None), P("chan", "cyl")),
        out_specs=P("cyl", "chan", None, None),
        check_vma=False,
    )
```

profile of v0, /device:TPU:1, one launch (start us, length us, event | category | flops | bytes accessed | tf_op | source)
XLA Modules:
  0.0 93.9 jit_solution(18110909361854007558)
XLA Ops:
  0.0 1.1 %dynamic-slice_bitcast_fusion = bf16[8,2,1,16,512]{4,3,1,0,2:T(8,128)(2,1)S(1)} fusion(bf16[8,2,2,64,512]{4,3,2,1,0:T(8,128)(2,1)} %refs_1_.7, s32[]{:T(128)S(6)} %select_n.20), kind=kLoop, calls=%fused_computation | loop fusion | bytes 524292 | tf_op jit(solution)/shard_map/optimization_barrier | solution.py:187
  1.1 1.7 %constant_dynamic-slice_fusion.2 = bf16[8,2,1,16,512]{4,3,1,0,2:T(8,128)(2,1)} fusion(s32[]{:T(128)S(6)} %select_n.21, bf16[8,2,2,64,512]{4,3,2,1,0:T(8,128)(2,1)} %refs_1_.7), kind=kLoop, calls=%fused_computation.8 | loop fusion | bytes 524292 | tf_op jit(solution)/shard_map/dynamic_slice | solution.py:186
  2.8 7.7 %collective-permute-start.2 = (bf16[8,2,16,512]{3,2,1,0:T(8,128)(2,1)}, bf16[8,2,16,512]{3,2,1,0:T(8,128)(2,1)S(1)}, u32[]{:S(2)}, u32[]{:S(2)}) collective-permute-start(bf16[8,2,16,512]{3,2,1,0:T(8,128)(2,1)} %bitcast.3), channel_id=1, source_target_pairs={{0,1},{1,0},{2,3},{3,2},{4,5},{5,4},{6,7},{7,6},{8,9},{9,8},{10,11... | collective-permute-start | bytes 786440 | tf_op jit(solution)/shard_map/ppermute | solution.py:188
  10.6 0.0 collective-permute-start.3
  10.6 1.7 %constant_dynamic-slice_fusion.1 = bf16[8,2,1,16,512]{4,3,1,0,2:T(8,128)(2,1)} fusion(s32[]{:T(128)S(6)} %select_n.20, bf16[8,2,2,64,512]{4,3,2,1,0:T(8,128)(2,1)} %refs_1_.7), kind=kLoop, calls=%fused_computation.7 | loop fusion | bytes 524292 | tf_op jit(solution)/shard_map/dynamic_slice | solution.py:186
  12.3 5.3 %collective-permute-start.1 = (bf16[8,2,16,512]{3,2,1,0:T(8,128)(2,1)}, bf16[8,2,16,512]{3,2,1,0:T(8,128)(2,1)S(1)}, u32[]{:S(2)}, u32[]{:S(2)}) collective-permute-start(bf16[8,2,16,512]{3,2,1,0:T(8,128)(2,1)} %bitcast.2), channel_id=1, source_target_pairs={{0,1},{1,0},{2,3},{3,2},{4,5},{5,4},{6,7},{7,6},{8,9},{9,8},{10,11... | collective-permute-start | bytes 786440 | tf_op jit(solution)/shard_map/ppermute | solution.py:188
  17.6 1.7 %constant_dynamic-slice_fusion = bf16[8,2,1,16,512]{4,3,1,0,2:T(8,128)(2,1)} fusion(s32[]{:T(128)S(6)} %select_n.21, bf16[8,2,2,64,512]{4,3,2,1,0:T(8,128)(2,1)} %refs_1_.7), kind=kLoop, calls=%fused_computation.6 | loop fusion | bytes 524292 | tf_op jit(solution)/shard_map/dynamic_slice | solution.py:186
  19.3 0.0 collective-permute-start
  19.3 5.3 %collective-permute-start.4 = (s32[8,2]{0,1:T(2,128)S(1)}, s32[8,2]{0,1:T(2,128)S(1)}, u32[]{:S(2)}, u32[]{:S(2)}) collective-permute-start(s32[8,2]{0,1:T(2,128)S(1)} %copy-done.4), channel_id=1, source_target_pairs={{0,1},{1,0},{2,3},{3,2},{4,5},{5,4},{6,7},{7,6},{8,9},{9,8},{10,11... | collective-permute-start | bytes 200 | tf_op jit(solution)/shard_map/ppermute | solution.py:189
  24.7 14.6 %collective-permute-done.4 = s32[8,2]{0,1:T(2,128)S(1)} collective-permute-done((s32[8,2]{0,1:T(2,128)S(1)}, s32[8,2]{0,1:T(2,128)S(1)}, u32[]{:S(2)}, u32[]{:S(2)}) %collective-permute-start.4) | collective-permute-done | bytes 96 | tf_op jit(solution)/shard_map/ppermute | solution.py:189
  39.2 0.1 broadcast_in_dim.3
  39.3 0.1 reshape.35.refs_6_
  39.4 0.0 collective-permute-done.3.refs_2_
  39.4 0.0 copy-start.1
  39.4 1.0 %copy-done.1 = bf16[512,512]{1,0:T(8,128)(2,1)S(1)} copy-done((bf16[512,512]{1,0:T(8,128)(2,1)S(1)}, bf16[512,512]{1,0:T(8,128)(2,1)}, u32[]{:S(2)}) %copy-start.1) | copy-done | bytes 524312
  40.5 0.9 copy-done.3
  41.4 1.4 %beam_step.3.refs_5_ = f32[4,256,128]{2,1,0:T(8,128)S(1)} custom-call(s32[1]{0:T(128)} %bitcast.refs_0_, bf16[8,2,2,64,512]{4,3,2,1,0:T(8,128)(2,1)S(1)} %copy-done, bf16[8,2,16,512]{3,2,1,0:T(8,128)(2,1)S(1)} %collective-permute-done.3.refs_2_, bf16[512,512]{1,0:T(8,128)(2,1)S(1)} %copy-done.1, bf16[256,256]{1,0:T(8,128)(2,1)S(1)} %copy-done.3), custom_call_target="tpu_custom_call" | custom-call | flops 402653184 | bytes 2097152 | tf_op jit(solution)/shard_map/beam_step/pallas_call | solution.py:142
  42.7 0.0 collective-permute-done.2.refs_2_
  42.8 1.4 %beam_step.4.refs_5_ = f32[4,256,128]{2,1,0:T(8,128)S(1)} custom-call(s32[1]{0:T(128)} %bitcast.refs_0_, bf16[8,2,2,64,512]{4,3,2,1,0:T(8,128)(2,1)S(1)} %copy-done, bf16[8,2,16,512]{3,2,1,0:T(8,128)(2,1)S(1)} %collective-permute-done.2.refs_2_, bf16[512,512]{1,0:T(8,128)(2,1)S(1)} %copy-done.2, ...), custom_call_target="tpu_custom_call", output_to_operand_aliasing={{}: (5, {})} | custom-call | flops 402653184 | bytes 2097152 | tf_op jit(solution)/shard_map/beam_step/pallas_call | solution.py:142
  44.2 0.0 collective-permute-done.1.refs_2_
  44.2 1.4 %beam_step.5.refs_5_ = f32[4,256,128]{2,1,0:T(8,128)S(1)} custom-call(s32[1]{0:T(128)} %bitcast.refs_0_, bf16[8,2,2,64,512]{4,3,2,1,0:T(8,128)(2,1)S(1)} %copy-done, bf16[8,2,16,512]{3,2,1,0:T(8,128)(2,1)S(1)} %collective-permute-done.1.refs_2_, bf16[512,512]{1,0:T(8,128)(2,1)S(1)} %copy-done.2, ...), custom_call_target="tpu_custom_call", output_to_operand_aliasing={{}: (5, {})} | custom-call | flops 402653184 | bytes 2097152 | tf_op jit(solution)/shard_map/beam_step/pallas_call | solution.py:142
  45.6 1.4 %beam_step_last.1 = bf16[1024,128]{1,0:T(8,128)(2,1)S(1)} custom-call(s32[1]{0:T(128)} %bitcast.refs_0_, bf16[8,2,2,64,512]{4,3,2,1,0:T(8,128)(2,1)S(1)} %copy-done, bf16[8,2,16,512]{3,2,1,0:T(8,128)(2,1)S(1)} %collective-permute-done.refs_2_, bf16[512,512]{1,0:T(8,128)(2,1)S(1)} %copy-done.2, bf16[256,256]{1,0:T(8,128)(2,1)S(1)} %copy-done.3, ...), custom_call_target="tpu_custom_call" | custom-call | flops 402653184 | bytes 2097152 | tf_op jit(solution)/shard_map/beam_step_last/pallas_call | solution.py:142
  47.0 46.1 %all_to_all.5 = bf16[256,4,128]{2,1,0:T(4,128)(2,1)S(1)} all-to-all(bf16[256,4,128]{2,1,0:T(4,128)(2,1)S(1)} %bitcast.16), channel_id=1, replica_groups=mesh['chan'=128,'cyl'=2] {'chan','cyl'}, dimensions={0} | all-to-all | bytes 524288 | tf_op jit(solution)/shard_map/all_to_all | solution.py:200
  93.1 0.9 place.1
  (10 shorter events, 0.0 us)
Async XLA Ops:
  0.0 39.4 %copy-start = (bf16[8,2,2,64,512]{4,3,2,1,0:T(8,128)(2,1)S(1)}, bf16[8,2,2,64,512]{4,3,2,1,0:T(8,128)(2,1)}, u32[]{:S(2)}) copy-start(bf16[8,2,2,64,512]{4,3,2,1,0:T(8,128)(2,1)} %refs_1_.7) | copy-start | bytes 6291460
  0.0 19.3 %copy-start.4 = (s32[8,2]{0,1:T(2,128)S(1)}, s32[8,2]{0,1:T(2,128)}, u32[]{:S(2)}) copy-start(s32[8,2]{0,1:T(2,128)} %param.5) | copy-start | bytes 196
  2.8 39.9 %collective-permute-start.2 = (bf16[8,2,16,512]{3,2,1,0:T(8,128)(2,1)}, bf16[8,2,16,512]{3,2,1,0:T(8,128)(2,1)S(1)}, u32[]{:S(2)}, u32[]{:S(2)}) collective-permute-start(bf16[8,2,16,512]{3,2,1,0:T(8,128)(2,1)} %bitcast.3), channel_id=1, source_target_pairs={{0,1},{1,0},{2,3},{3,2},{4,5},{5,4},{6,7},{7,6},{8,9},{9,8},{10,11... | collective-permute-start | bytes 786440 | tf_op jit(solution)/shard_map/ppermute | solution.py:188
  10.6 28.8 %collective-permute-start.3 = (bf16[8,2,16,512]{3,2,1,0:T(8,128)(2,1)S(1)}, bf16[8,2,16,512]{3,2,1,0:T(8,128)(2,1)S(1)}, u32[]{:S(2)}, u32[]{:S(2)}) collective-permute-start(bf16[8,2,16,512]{3,2,1,0:T(8,128)(2,1)S(1)} %bitcast.18), channel_id=1, source_target_pairs={{0,1},{1,0},{2,3},{3,2},{4,5},{5,4},{6,7},{7,6},{8,9},{9,8},{10,11... | collective-permute-start | bytes 786440 | tf_op jit(solution)/shard_map/ppermute | solution.py:188
  12.3 31.9 %collective-permute-start.1 = (bf16[8,2,16,512]{3,2,1,0:T(8,128)(2,1)}, bf16[8,2,16,512]{3,2,1,0:T(8,128)(2,1)S(1)}, u32[]{:S(2)}, u32[]{:S(2)}) collective-permute-start(bf16[8,2,16,512]{3,2,1,0:T(8,128)(2,1)} %bitcast.2), channel_id=1, source_target_pairs={{0,1},{1,0},{2,3},{3,2},{4,5},{5,4},{6,7},{7,6},{8,9},{9,8},{10,11... | collective-permute-start | bytes 786440 | tf_op jit(solution)/shard_map/ppermute | solution.py:188
  19.3 26.3 %collective-permute-start = (bf16[8,2,16,512]{3,2,1,0:T(8,128)(2,1)}, bf16[8,2,16,512]{3,2,1,0:T(8,128)(2,1)S(1)}, u32[]{:S(2)}, u32[]{:S(2)}) collective-permute-start(bf16[8,2,16,512]{3,2,1,0:T(8,128)(2,1)} %bitcast.1), channel_id=1, source_target_pairs={{0,1},{1,0},{2,3},{3,2},{4,5},{5,4},{6,7},{7,6},{8,9},{9,8},{10,11... | collective-permute-start | bytes 786440 | tf_op jit(solution)/shard_map/ppermute | solution.py:188
  19.3 19.9 %collective-permute-start.4 = (s32[8,2]{0,1:T(2,128)S(1)}, s32[8,2]{0,1:T(2,128)S(1)}, u32[]{:S(2)}, u32[]{:S(2)}) collective-permute-start(s32[8,2]{0,1:T(2,128)S(1)} %copy-done.4), channel_id=1, source_target_pairs={{0,1},{1,0},{2,3},{3,2},{4,5},{5,4},{6,7},{7,6},{8,9},{9,8},{10,11... | collective-permute-start | bytes 200 | tf_op jit(solution)/shard_map/ppermute | solution.py:189
  39.4 1.0 %copy-start.1 = (bf16[512,512]{1,0:T(8,128)(2,1)S(1)}, bf16[512,512]{1,0:T(8,128)(2,1)}, u32[]{:S(2)}) copy-start(bf16[512,512]{1,0:T(8,128)(2,1)} %constant.27.clone.refs_3_) | copy-start | bytes 1572868
  40.5 0.9 copy-start.3
  41.4 1.4 %copy-start.2 = (bf16[512,512]{1,0:T(8,128)(2,1)S(1)}, bf16[512,512]{1,0:T(8,128)(2,1)}, u32[]{:S(2)}) copy-start(bf16[512,512]{1,0:T(8,128)(2,1)} %constant.27.clone.refs_3_) | copy-start | bytes 1572868
where the time goes:
time: 94.2 us; the launch traced here: 93.9 us
  blocking collectives  46.1 us (49%)
  starting transfers between devices  18.5 us (20%)
  waiting for transfers between devices  14.6 us (15%)
  local copies, waits for them, and re-layouts  8.27 us (9%)
  Pallas kernels  6.44 us (7%)
    all_to_all x1, blocking collectives, local(): lax.all_to_all(sent, ('chan', 'cyl'), split_axis=0, concat_axis=0, tiled=...  46.1 us
    ppermute x1, waiting for transfers between devices, local(): others = lax.ppermute(gain_exponents, 'cyl', pair)  14.6 us
    ppermute x4, starting transfers between devices, local(): lax.ppermute(piece.reshape(chans, cyls, UP, 2 * FEEDS), 'cyl', pair)  13.1 us
    pallas_call x4, Pallas kernels, step(): pl.pallas_call(lambda *refs: step_kernel(first, last, *refs), out_shape=o...  5.57 us
    ppermute x1, starting transfers between devices, local(): others = lax.ppermute(gain_exponents, 'cyl', pair)  5.34 us
    dynamic_slice x3, local copies, waits for them, and re-layouts, local(): lax.dynamic_slice(source, (0, 0, pol, start, 0), (chans, cyls, 1, UP, 2 *...  5.03 us
    unnamed x10, local copies, waits for them, and re-layouts  1.95 us
  transfers between devices with their start and end apart: 5, of which 1 were waited for; matrix products, arithmetic and copies ran while one was open for 4% of the time, Pallas kernels for 4%

commit v1 on v0

--- a/solution.py
+++ b/solution.py
@@ -72,12 +72,28 @@
     ]
 
 
+def gain_rows(k, own_ref, other_ref):
+    own = own_ref[...].astype(jnp.float32)
+    other = other_ref[...].astype(jnp.float32)
+    chans = own.shape[0]
+    lane = lax.broadcasted_iota(jnp.int32, (chans, LANES), 1)
+    chan = lax.broadcasted_iota(jnp.int32, (chans, LANES), 0)
+    hit = lane // UP == chan
+    rows = []
+    for pair in (jnp.where(k == 0, own, other), jnp.where(k == 0, other, own)):
+        for beam in range(2):
+            gain = jnp.broadcast_to(pair[:, beam : beam + 1], (chans, LANES))
+            row = jnp.sum(jnp.where(hit, gain, 0.0), axis=0, keepdims=True)
+            rows.append(jnp.exp2(2.0 * row) / (POLS * SUMS))
+    return rows
+
+
 def step_kernel(first, last, *refs):
     refs = list(refs)
     k_ref, own_ref, recv_ref, t_ref, u_ref = refs[:5]
     refs = refs[5:]
     acc_in = None if first else refs.pop(0)
-    scale_ref = refs.pop(0) if last else None
+    gain_refs = [refs.pop(0), refs.pop(0)] if last else None
     out_ref = refs.pop(0)
     x_ref = refs.pop(0)
     stage_ref = refs.pop(0) if last else None
@@ -87,6 +103,8 @@
         other = pl.ds(pl.multiple_of((2 * (1 - k) + cyl) * LANES, LANES), LANES)
         x_ref[mine, :] = own_ref[:, cyl, 0].reshape(LANES, 2 * FEEDS)
         x_ref[other, :] = recv_ref[:, cyl].reshape(LANES, 2 * FEEDS)
+    if last:
+        scale = gain_rows(k, *gain_refs)
     dims = (((1,), (1,)), ((), ()))
     half = FEEDS // 2
     for low in range(2):
@@ -105,14 +123,14 @@
             if not first:
                 power = acc_in[e, rows, :] + power
             if last:
-                stage_ref[pl.ds(2 * e + low, half, stride=8), :] = power * scale_ref[pl.ds(e, 1), :]
+                stage_ref[pl.ds(2 * e + low, half, stride=8), :] = power * scale[e]
             else:
                 out_ref[e, rows, :] = power
     if last:
         out_ref[...] = stage_ref[...].astype(jnp.bfloat16)
 
 
-def step(pol, block, first, last, k, volts, recv, table, up_table, acc, scale):
+def step(pol, block, first, last, k, volts, recv, table, up_table, acc, gains):
     chans, cyls = volts.shape[:2]
     whole = lambda a: pl.BlockSpec(a.shape, lambda i, kk: (0,) * a.ndim)
     args = [volts, recv, table, up_table]
@@ -130,8 +148,8 @@
         args.append(acc)
         specs.append(whole(acc))
     if last:
-        args.append(scale)
-        specs.append(whole(scale))
+        args.extend(gains)
+        specs.extend(whole(g) for g in gains)
         out = jax.ShapeDtypeStruct((FEEDS * CYLS, LANES), jnp.bfloat16)
     else:
         out = jax.ShapeDtypeStruct((CYLS, FEEDS, LANES), jnp.float32)
@@ -151,9 +169,41 @@
         ),
         input_output_aliases=aliases,
         cost_estimate=pl.CostEstimate(flops=flops, bytes_accessed=2 << 20, transcendentals=0),
-        compiler_params=pltpu.CompilerParams(vmem_limit_bytes=24 << 20),
+        compiler_params=pltpu.CompilerParams(vmem_limit_bytes=8 << 20),
         name="beam_step_last" if last else "beam_step",
     )(k, *args)
+
+
+def split_kernel(steps, k_ref, volts_ref, *refs):
+    outs, sems = refs[:-1], refs[-1]
+    start = (1 - k_ref[0]) * (SUMS * UP)
+    copies = []
+    for index, (pol, block) in enumerate(steps):
+        rows = pl.ds(pl.multiple_of(start + block * UP, UP), UP)
+        copies.append(pltpu.make_async_copy(volts_ref.at[:, :, pol, rows, :], outs[index], sems.at[index]))
+    for copy in copies:
+        copy.start()
+    for copy in copies:
+        copy.wait()
+
+
+def split(volts, which, steps):
+    chans, cyls = volts.shape[:2]
+    piece = jax.ShapeDtypeStruct((chans, cyls, UP, 2 * FEEDS), volts.dtype)
+    count = len(steps)
+    return pl.pallas_call(
+        lambda *refs: split_kernel(steps, *refs),
+        out_shape=[piece] * count,
+        grid_spec=pltpu.PrefetchScalarGridSpec(
+            num_scalar_prefetch=1,
+            grid=(1,),
+            in_specs=[pl.BlockSpec(memory_space=pltpu.HBM)],
+            out_specs=[pl.BlockSpec(memory_space=pltpu.VMEM)] * count,
+            scratch_shapes=[pltpu.SemaphoreType.DMA((count,))],
+        ),
+        compiler_params=pltpu.CompilerParams(vmem_limit_bytes=2 << 20),
+        name="split",
+    )(which, volts)
 
 
 def place_kernel(in_ref, out_ref, wide_ref):
@@ -167,7 +217,7 @@
         place_kernel,
         out_shape=jax.ShapeDtypeStruct((4, 256, LANES), jnp.float32),
         scratch_shapes=[pltpu.VMEM((1024, LANES), jnp.float32)],
-        compiler_params=pltpu.CompilerParams(vmem_limit_bytes=24 << 20),
+        compiler_params=pltpu.CompilerParams(vmem_limit_bytes=8 << 20),
         name="place",
     )(arrived)
 
@@ -179,23 +229,15 @@
     table = jnp.asarray(ns_rows(FEEDS))
     up_table = jnp.asarray(up_columns(UP, chans))
     steps = [(pol, block) for pol in range(POLS) for block in range(SUMS)]
-    received = []
-    source = volts
-    for pol, block in steps:
-        start = (1 - k) * (SUMS * UP) + block * UP
-        piece = lax.dynamic_slice(source, (0, 0, pol, start, 0), (chans, cyls, 1, UP, 2 * FEEDS))
-        source, piece = lax.optimization_barrier((source, piece))
-        received.append(lax.ppermute(piece.reshape(chans, cyls, UP, 2 * FEEDS), "cyl", pair))
+    which = k.astype(jnp.int32).reshape(1)
+    source = pltpu.with_memory_space_constraint(volts, pltpu.HBM)
+    pieces = split(source, which, steps[:1]) + split(source, which, steps[1:])
+    received = [lax.ppermute(piece, "cyl", pair) for piece in pieces]
     others = lax.ppermute(gain_exponents, "cyl", pair)
-    low = jnp.where(k == 0, gain_exponents, others)
-    high = jnp.where(k == 0, others, gain_exponents)
-    gains = jnp.exp2(2.0 * jnp.concatenate([low, high], axis=1).astype(jnp.float32)) / (POLS * SUMS)
-    scale = jnp.repeat(gains.T, UP, axis=1)
-    which = k.astype(jnp.int32).reshape(1)
     acc = None
     for index, (pol, block) in enumerate(steps):
         first, last = index == 0, index == len(steps) - 1
-        acc = step(pol, block, first, last, which, volts, received[index], table, up_table, acc, scale)
+        acc = step(pol, block, first, last, which, volts, received[index], table, up_table, acc, (gain_exponents, others))
     sent = acc.reshape(256, 4, LANES)
     arrived = lax.all_to_all(sent, ("chan", "cyl"), split_axis=0, concat_axis=0, tiled=True)
     placed = place(arrived.reshape(1024, LANES))

time: 94.2 us -> 86.3 us (0.916)
  blocking collectives: 46.1 us -> 36.2 us
  local copies, waits for them, and re-layouts: 8.27 us -> 0.1 us
  waiting for transfers between devices: 14.6 us -> 19.7 us
  Pallas kernels: 6.44 us -> 11.4 us
    all_to_all x1, blocking collectives: 46.1 us -> 36.2 us  [local(): lax.all_to_all(sent, ('chan', 'cyl'), split_axis=0, concat_axis=0, tiled=...]
    ppermute x4, waiting for transfers between devices: 0.01 us -> 8.28 us  [local(): received = [lax.ppermute(piece, 'cyl', pair) for piece in pieces]]
    dynamic_slice x3 -> x0, local copies, waits for them, and re-layouts: 5.03 us -> none  [local(): lax.dynamic_slice(source, (0, 0, pol, start, 0), (chans, cyls, 1, UP, 2 *...]
    ppermute x1, waiting for transfers between devices: 14.6 us -> 11.4 us  [local(): others = lax.ppermute(gain_exponents, 'cyl', pair)]
    pallas_call x0 -> x2, Pallas kernels: none -> 3.12 us  [split(): pl.pallas_call(lambda *refs: split_kernel(steps, *refs), out_shape=[piece...]
    pallas_call x4, Pallas kernels: 5.57 us -> 7.42 us  [step(): pl.pallas_call(lambda *refs: step_kernel(first, last, *refs), out_shape=o...]
    unnamed x10 -> x9, local copies, waits for them, and re-layouts: 1.95 us -> 0.1 us
    optimization_barrier x1 -> x0, local copies, waits for them, and re-layouts: 1.13 us -> none  [local(): source, piece = lax.optimization_barrier((source, piece))]
  transfers between devices with their start and end apart: 5 -> 5, of which waited for: 1 -> 3; matrix products, arithmetic and copies ran while one was open for 4% -> 0% of each run, Pallas kernels for 4% -> 9%
where the time goes in v1:
time: 86.3 us; the launch traced here: 86.1 us
  blocking collectives  36.2 us (42%)
  waiting for transfers between devices  19.7 us (23%)
  starting transfers between devices  18.7 us (22%)
  Pallas kernels  11.4 us (13%)
    all_to_all x1, blocking collectives, local(): lax.all_to_all(sent, ('chan', 'cyl'), split_axis=0, concat_axis=0, tiled=...  36.2 us
    ppermute x4, starting transfers between devices, local(): received = [lax.ppermute(piece, 'cyl', pair) for piece in pieces]  13.4 us
    ppermute x1, waiting for transfers between devices, local(): others = lax.ppermute(gain_exponents, 'cyl', pair)  11.4 us
    ppermute x4, waiting for transfers between devices, local(): received = [lax.ppermute(piece, 'cyl', pair) for piece in pieces]  8.28 us
    pallas_call x4, Pallas kernels, step(): pl.pallas_call(lambda *refs: step_kernel(first, last, *refs), out_shape=o...  7.42 us
    ppermute x1, starting transfers between devices, local(): others = lax.ppermute(gain_exponents, 'cyl', pair)  5.28 us
    pallas_call x2, Pallas kernels, split(): pl.pallas_call(lambda *refs: split_kernel(steps, *refs), out_shape=[piece...  3.12 us
  transfers between devices with their start and end apart: 5, of which 3 were waited for; matrix products, arithmetic and copies ran while one was open for 0% of the time, Pallas kernels for 9%

profile of v1, /device:TPU:1, one launch (start us, length us, event | category | flops | bytes accessed | tf_op | source)
XLA Modules:
  0.0 86.1 jit_solution(16365951834275720502)
XLA Ops:
  0.0 0.0 copy-start.2
  0.0 1.1 %split.3 = bf16[8,2,16,512]{3,2,1,0:T(8,128)(2,1)S(1)} custom-call(s32[1]{0:T(128)} %bitcast.refs_0_, bf16[8,2,2,64,512]{4,3,2,1,0:T(8,128)(2,1)} %refs_1_.11), custom_call_target="tpu_custom_call" | custom-call | tf_op jit(solution)/shard_map/split/pallas_call | solution.py:194
  1.1 7.8 %collective-permute-start.3 = (bf16[8,2,16,512]{3,2,1,0:T(8,128)(2,1)S(1)}, bf16[8,2,16,512]{3,2,1,0:T(8,128)(2,1)}, u32[]{:S(2)}, u32[]{:S(2)}) collective-permute-start(bf16[8,2,16,512]{3,2,1,0:T(8,128)(2,1)S(1)} %split.3), channel_id=1, source_target_pairs={{0,1},{1,0},{2,3},{3,2},{4,5},{5,4},{6,7},{7,6},{8,9},{9,8},{10,11... | collective-permute-start | bytes 786440 | tf_op jit(solution)/shard_map/ppermute | solution.py:235
  9.0 2.0 %split.2 = (bf16[8,2,16,512]{3,2,1,0:T(8,128)(2,1)}, bf16[8,2,16,512]{3,2,1,0:T(8,128)(2,1)}, bf16[8,2,16,512]{3,2,1,0:T(8,128)(2,1)}) custom-call(s32[1]{0:T(128)} %bitcast.refs_0_, bf16[8,2,2,64,512]{4,3,2,1,0:T(8,128)(2,1)} %refs_1_.11), custom_call_target="tpu_custom_call" | custom-call | tf_op jit(solution)/shard_map/split/pallas_call | solution.py:194
  11.0 0.1 collective-permute-start.2
  11.1 5.4 %collective-permute-start.1 = (bf16[8,2,16,512]{3,2,1,0:T(8,128)(2,1)}, bf16[8,2,16,512]{3,2,1,0:T(8,128)(2,1)S(1)}, u32[]{:S(2)}, u32[]{:S(2)}) collective-permute-start(bf16[8,2,16,512]{3,2,1,0:T(8,128)(2,1)} %get-tuple-element.9), channel_id=1, source_target_pairs={{0,1},{1,0},{2,3},{3,2},{4,5},{5,4},{6,7},{7,6},{8,9},{9,8},{10,11... | collective-permute-start | bytes 786440 | tf_op jit(solution)/shard_map/ppermute | solution.py:235
  16.4 0.1 collective-permute-start
  16.5 0.0 copy-done.3
  16.6 0.1 copy.8.refs_6_
  16.6 5.3 %collective-permute-start.4 = (s32[8,2]{1,0:T(8,128)S(1)}, s32[8,2]{1,0:T(8,128)S(1)}, u32[]{:S(2)}, u32[]{:S(2)}) collective-permute-start(s32[8,2]{1,0:T(8,128)S(1)} %copy.8.refs_6_), channel_id=1, source_target_pairs={{0,1},{1,0},{2,3},{3,2},{4,5},{5,4},{6,7},{7,6},{8,9},{9,8},{10,11... | collective-permute-start | bytes 200 | tf_op jit(solution)/shard_map/ppermute | solution.py:236
  21.9 0.0 collective-permute-done.3.refs_2_
  21.9 0.0 copy-done
  21.9 0.0 copy-done.1
  21.9 0.0 copy-done.2
  21.9 2.3 %beam_step.3.refs_5_ = f32[4,256,128]{2,1,0:T(8,128)S(1)} custom-call(s32[1]{0:T(128)} %bitcast.refs_0_, bf16[8,2,2,64,512]{4,3,2,1,0:T(8,128)(2,1)S(1)} %copy-done, bf16[8,2,16,512]{3,2,1,0:T(8,128)(2,1)} %collective-permute-done.3.refs_2_, bf16[512,512]{1,0:T(8,128)(2,1)S(1)} %copy-done.1, bf16[256,256]{1,0:T(8,128)(2,1)S(1)} %copy-done.2), custom_call_target="tpu_custom_call" | custom-call | flops 402653184 | bytes 2097152 | tf_op jit(solution)/shard_map/beam_step/pallas_call | solution.py:160
  24.2 0.1 collective-permute-done.2.refs_2_
  24.3 2.3 %beam_step.4.refs_5_ = f32[4,256,128]{2,1,0:T(8,128)S(1)} custom-call(s32[1]{0:T(128)} %bitcast.refs_0_, bf16[8,2,2,64,512]{4,3,2,1,0:T(8,128)(2,1)S(1)} %copy-done, bf16[8,2,16,512]{3,2,1,0:T(8,128)(2,1)} %collective-permute-done.2.refs_2_, bf16[512,512]{1,0:T(8,128)(2,1)S(1)} %copy-done.1, ...), custom_call_target="tpu_custom_call", output_to_operand_aliasing={{}: (5, {})} | custom-call | flops 402653184 | bytes 2097152 | tf_op jit(solution)/shard_map/beam_step/pallas_call | solution.py:160
  26.7 8.2 %collective-permute-done.1.refs_2_ = bf16[8,2,16,512]{3,2,1,0:T(8,128)(2,1)S(1)} collective-permute-done((bf16[8,2,16,512]{3,2,1,0:T(8,128)(2,1)}, bf16[8,2,16,512]{3,2,1,0:T(8,128)(2,1)S(1)}, u32[]{:S(2)}, u32[]{:S(2)}) %collective-permute-start.1) | collective-permute-done | bytes 262176 | tf_op jit(solution)/shard_map/ppermute | solution.py:235
  34.9 1.4 %beam_step.5.refs_5_ = f32[4,256,128]{2,1,0:T(8,128)S(1)} custom-call(s32[1]{0:T(128)} %bitcast.refs_0_, bf16[8,2,2,64,512]{4,3,2,1,0:T(8,128)(2,1)S(1)} %copy-done, bf16[8,2,16,512]{3,2,1,0:T(8,128)(2,1)S(1)} %collective-permute-done.1.refs_2_, bf16[512,512]{1,0:T(8,128)(2,1)S(1)} %copy-done.1, ...), custom_call_target="tpu_custom_call", output_to_operand_aliasing={{}: (5, {})} | custom-call | flops 402653184 | bytes 2097152 | tf_op jit(solution)/shard_map/beam_step/pallas_call | solution.py:160
  36.3 11.4 %collective-permute-done.4.refs_7_ = s32[8,2]{1,0:T(8,128)S(1)} collective-permute-done((s32[8,2]{1,0:T(8,128)S(1)}, s32[8,2]{1,0:T(8,128)S(1)}, u32[]{:S(2)}, u32[]{:S(2)}) %collective-permute-start.4) | collective-permute-done | bytes 96 | tf_op jit(solution)/shard_map/ppermute | solution.py:236
  47.6 0.0 collective-permute-done.refs_2_
  47.6 1.4 %beam_step_last.1 = bf16[1024,128]{1,0:T(8,128)(2,1)S(1)} custom-call(s32[1]{0:T(128)} %bitcast.refs_0_, bf16[8,2,2,64,512]{4,3,2,1,0:T(8,128)(2,1)S(1)} %copy-done, bf16[8,2,16,512]{3,2,1,0:T(8,128)(2,1)S(1)} %collective-permute-done.refs_2_, bf16[512,512]{1,0:T(8,128)(2,1)S(1)} %copy-done.1, bf16[256,256]{1,0:T(8,128)(2,1)S(1)} %copy-done.2, ...), custom_call_target="tpu_custom_call" | custom-call | flops 402653184 | bytes 2097152 | tf_op jit(solution)/shard_map/beam_step_last/pallas_call | solution.py:160
  49.0 36.2 %all_to_all.5 = bf16[256,4,128]{2,1,0:T(4,128)(2,1)S(1)} all-to-all(bf16[256,4,128]{2,1,0:T(4,128)(2,1)S(1)} %bitcast.8), channel_id=1, replica_groups=mesh['chan'=128,'cyl'=2] {'chan','cyl'}, dimensions={0} | all-to-all | bytes 524288 | tf_op jit(solution)/shard_map/all_to_all | solution.py:242
  85.2 0.9 %place.1 = f32[4,256,128]{2,1,0:T(8,128)} custom-call(bf16[1024,128]{1,0:T(8,128)(2,1)S(1)} %bitcast.9), custom_call_target="tpu_custom_call" | custom-call | tf_op jit(solution)/shard_map/place/pallas_call | solution.py:216
  (3 shorter events, 0.0 us)
Async XLA Ops:
  0.0 16.6 %copy-start.3 = (s32[8,2]{0,1:T(2,128)S(1)}, s32[8,2]{0,1:T(2,128)}, u32[]{:S(2)}) copy-start(s32[8,2]{0,1:T(2,128)} %param.5) | copy-start | bytes 196
  0.0 21.9 %copy-start = (bf16[8,2,2,64,512]{4,3,2,1,0:T(8,128)(2,1)S(1)}, bf16[8,2,2,64,512]{4,3,2,1,0:T(8,128)(2,1)}, u32[]{:S(2)}) copy-start(bf16[8,2,2,64,512]{4,3,2,1,0:T(8,128)(2,1)} %refs_1_.11) | copy-start | bytes 6291460
  0.0 21.9 %copy-start.1 = (bf16[512,512]{1,0:T(8,128)(2,1)S(1)}, bf16[512,512]{1,0:T(8,128)(2,1)}, u32[]{:S(2)}) copy-start(bf16[512,512]{1,0:T(8,128)(2,1)} %constant.8.clone.refs_3_) | copy-start | bytes 1572868
  0.0 21.9 %copy-start.2 = (bf16[256,256]{1,0:T(8,128)(2,1)S(1)}, bf16[256,256]{1,0:T(8,128)(2,1)}, u32[]{:S(2)}) copy-start(bf16[256,256]{1,0:T(8,128)(2,1)} %constant.9.clone.refs_4_) | copy-start | bytes 393220
  1.1 20.8 %collective-permute-start.3 = (bf16[8,2,16,512]{3,2,1,0:T(8,128)(2,1)S(1)}, bf16[8,2,16,512]{3,2,1,0:T(8,128)(2,1)}, u32[]{:S(2)}, u32[]{:S(2)}) collective-permute-start(bf16[8,2,16,512]{3,2,1,0:T(8,128)(2,1)S(1)} %split.3), channel_id=1, source_target_pairs={{0,1},{1,0},{2,3},{3,2},{4,5},{5,4},{6,7},{7,6},{8,9},{9,8},{10,11... | collective-permute-start | bytes 786440 | tf_op jit(solution)/shard_map/ppermute | solution.py:235
  11.0 13.4 %collective-permute-start.2 = (bf16[8,2,16,512]{3,2,1,0:T(8,128)(2,1)}, bf16[8,2,16,512]{3,2,1,0:T(8,128)(2,1)}, u32[]{:S(2)}, u32[]{:S(2)}) collective-permute-start(bf16[8,2,16,512]{3,2,1,0:T(8,128)(2,1)} %get-tuple-element.10), channel_id=1, source_target_pairs={{0,1},{1,0},{2,3},{3,2},{4,5},{5,4},{6,7},{7,6},{8,9},{9,8},{10,11... | collective-permute-start | bytes 786440 | tf_op jit(solution)/shard_map/ppermute | solution.py:235
  11.1 23.8 %collective-permute-start.1 = (bf16[8,2,16,512]{3,2,1,0:T(8,128)(2,1)}, bf16[8,2,16,512]{3,2,1,0:T(8,128)(2,1)S(1)}, u32[]{:S(2)}, u32[]{:S(2)}) collective-permute-start(bf16[8,2,16,512]{3,2,1,0:T(8,128)(2,1)} %get-tuple-element.9), channel_id=1, source_target_pairs={{0,1},{1,0},{2,3},{3,2},{4,5},{5,4},{6,7},{7,6},{8,9},{9,8},{10,11... | collective-permute-start | bytes 786440 | tf_op jit(solution)/shard_map/ppermute | solution.py:235
  16.4 31.2 %collective-permute-start = (bf16[8,2,16,512]{3,2,1,0:T(8,128)(2,1)}, bf16[8,2,16,512]{3,2,1,0:T(8,128)(2,1)S(1)}, u32[]{:S(2)}, u32[]{:S(2)}) collective-permute-start(bf16[8,2,16,512]{3,2,1,0:T(8,128)(2,1)} %get-tuple-element.8), channel_id=1, source_target_pairs={{0,1},{1,0},{2,3},{3,2},{4,5},{5,4},{6,7},{7,6},{8,9},{9,8},{10,11... | collective-permute-start | bytes 786440 | tf_op jit(solution)/shard_map/ppermute | solution.py:235
  16.6 31.0 %collective-permute-start.4 = (s32[8,2]{1,0:T(8,128)S(1)}, s32[8,2]{1,0:T(8,128)S(1)}, u32[]{:S(2)}, u32[]{:S(2)}) collective-permute-start(s32[8,2]{1,0:T(8,128)S(1)} %copy.8.refs_6_), channel_id=1, source_target_pairs={{0,1},{1,0},{2,3},{3,2},{4,5},{5,4},{6,7},{7,6},{8,9},{9,8},{10,11... | collective-permute-start | bytes 200 | tf_op jit(solution)/shard_map/ppermute | solution.py:236

commit v2 on v1

--- a/solution.py
+++ b/solution.py
@@ -39,37 +39,27 @@
     return np.block(table).astype(np.float32).astype(ml_dtypes.bfloat16)
 
 
-def rounded(value):
-    return value.astype(jnp.bfloat16).astype(jnp.float32)
-
-
-def ew_beams(real, imag):
-    s = math.sqrt(0.5) / 2.0
-    h0r, h0i = real[0] * 0.5, imag[0] * 0.5
-    n1r, n1i = real[1] * s, imag[1] * s
-    a1, b1 = n1r + n1i, n1r - n1i
-    h2r, h2i = real[2] * 0.5, imag[2] * 0.5
-    n3r, n3i = real[3] * s, imag[3] * s
-    a3, b3 = n3r + n3i, n3r - n3i
-    first = [
-        (h0r - a1, h0i + b1),
-        (h0r + b1, h0i + a1),
-        (h0r + a1, h0i - b1),
-        (h0r - b1, h0i - a1),
-    ]
-    second = [
-        (h2i + b3, a3 - h2r),
-        (-h2i - a3, h2r + b3),
-        (h2i - b3, -h2r - a3),
-        (a3 - h2i, h2r - b3),
-    ]
-    return [
-        (
-            (rounded(f[0]) + rounded(g[0])).astype(jnp.bfloat16),
-            (rounded(f[1]) + rounded(g[1])).astype(jnp.bfloat16),
-        )
-        for f, g in zip(first, second)
-    ]
+def ew_partials(real, imag, sign):
+    half = 0.5 * sign
+    diag = math.sqrt(0.5) / 2.0 * sign
+    hr, hi = real[0] * half, imag[0] * half
+    nr, ni = real[1] * diag, imag[1] * diag
+    a, b = nr + ni, nr - ni
+    beams = [(hr - a, hi + b), (hr + b, hi + a), (hr + a, hi - b), (hr - b, hi - a)]
+    return [(r.astype(jnp.bfloat16), i.astype(jnp.bfloat16)) for r, i in beams]
+
+
+def ns_partials(x, t_ref, low, sign):
+    dims = (((1,), (1,)), ((), ()))
+    half = FEEDS // 2
+    real = lax.dot_general(t_ref[pl.ds(low * half, half), :], x, dims, preferred_element_type=jnp.float32)
+    imag = lax.dot_general(t_ref[pl.ds(FEEDS + low * half, half), :], x, dims, preferred_element_type=jnp.float32)
+    cut = lambda v: [v[:, :LANES], v[:, LANES:]]
+    return ew_partials(cut(real), cut(imag), sign)
+
+
+def pair_rows(read):
+    return jnp.concatenate([read(cyl).reshape(LANES, 2 * FEEDS) for cyl in range(2)], axis=0)
 
 
 def gain_rows(k, own_ref, other_ref):
@@ -88,6 +78,39 @@
     return rows
 
 
+def own_kernel(k_ref, own_ref, t_ref, out_ref):
+    x = pair_rows(lambda cyl: own_ref[:, cyl, 0])
+    half = FEEDS // 2
+    for low in range(2):
+        for e, parts in enumerate(ns_partials(x, t_ref, low, 1.0)):
+            for part in range(2):
+                out_ref[0, e, part, pl.ds(low * half, half), :] = parts[part]
+
+
+def own_partials(volts, table, k):
+    chans, cyls = volts.shape[:2]
+    shape = (POLS * SUMS, CYLS, 2, FEEDS, LANES)
+    return pl.pallas_call(
+        own_kernel,
+        out_shape=jax.ShapeDtypeStruct(shape, jnp.bfloat16),
+        grid_spec=pltpu.PrefetchScalarGridSpec(
+            num_scalar_prefetch=1,
+            grid=(POLS * SUMS,),
+            in_specs=[
+                pl.BlockSpec(
+                    (chans, cyls, 1, UP, 2 * FEEDS),
+                    lambda i, kk: (0, 0, i // SUMS, SUMS * kk[0] + i % SUMS, 0),
+                ),
+                pl.BlockSpec(table.shape, lambda i, kk: (0, 0)),
+            ],
+            out_specs=pl.BlockSpec((1, *shape[1:]), lambda i, kk: (i, 0, 0, 0, 0)),
+        ),
+        cost_estimate=pl.CostEstimate(flops=4 * 2 * 512 * 512 * 256, bytes_accessed=4 << 20, transcendentals=0),
+        compiler_params=pltpu.CompilerParams(vmem_limit_bytes=8 << 20),
+        name="own_partials",
+    )(k, volts, table)
+
+
 def step_kernel(first, last, *refs):
     refs = list(refs)
     k_ref, own_ref, recv_ref, t_ref, u_ref = refs[:5]
@@ -95,28 +118,24 @@
     acc_in = None if first else refs.pop(0)
     gain_refs = [refs.pop(0), refs.pop(0)] if last else None
     out_ref = refs.pop(0)
-    x_ref = refs.pop(0)
     stage_ref = refs.pop(0) if last else None
     k = k_ref[0]
-    for cyl in range(2):
-        mine = pl.ds(pl.multiple_of((2 * k + cyl) * LANES, LANES), LANES)
-        other = pl.ds(pl.multiple_of((2 * (1 - k) + cyl) * LANES, LANES), LANES)
-        x_ref[mine, :] = own_ref[:, cyl, 0].reshape(LANES, 2 * FEEDS)
-        x_ref[other, :] = recv_ref[:, cyl].reshape(LANES, 2 * FEEDS)
     if last:
         scale = gain_rows(k, *gain_refs)
-    dims = (((1,), (1,)), ((), ()))
+    sign = (1 - 2 * k).astype(jnp.float32)
+    x = pair_rows(lambda cyl: recv_ref[:, cyl])
     half = FEEDS // 2
     for low in range(2):
-        x = x_ref[...]
         rows = pl.ds(low * half, half)
-        real = lax.dot_general(t_ref[rows, :], x, dims, preferred_element_type=jnp.float32)
-        rows_i = pl.ds(FEEDS + low * half, half)
-        imag = lax.dot_general(t_ref[rows_i, :], x, dims, preferred_element_type=jnp.float32)
-        cut = lambda v: [v[:, c * LANES : (c + 1) * LANES] for c in range(CYLS)]
-        coded = ew_beams(cut(real), cut(imag))
-        for e in range(CYLS):
-            both = jnp.concatenate(coded[e], axis=1)
+        for e, (other_r, other_i) in enumerate(ns_partials(x, t_ref, low, sign)):
+            own_r = own_ref[0, e, 0, rows, :].astype(jnp.float32)
+            own_i = own_ref[0, e, 1, rows, :].astype(jnp.float32)
+            other_r, other_i = other_r.astype(jnp.float32), other_i.astype(jnp.float32)
+            if e % 2 == 0:
+                coded = own_r + other_i, own_i - other_r
+            else:
+                coded = own_r - other_i, own_i + other_r
+            both = jnp.concatenate([part.astype(jnp.bfloat16) for part in coded], axis=1)
             spectra = jnp.dot(both, u_ref[...], preferred_element_type=jnp.float32)
             squared = spectra * spectra
             power = squared[:, :LANES] + squared[:, LANES:]
@@ -130,14 +149,11 @@
         out_ref[...] = stage_ref[...].astype(jnp.bfloat16)
 
 
-def step(pol, block, first, last, k, volts, recv, table, up_table, acc, gains):
-    chans, cyls = volts.shape[:2]
+def step(index, first, last, k, own, recv, table, up_table, acc, gains):
     whole = lambda a: pl.BlockSpec(a.shape, lambda i, kk: (0,) * a.ndim)
-    args = [volts, recv, table, up_table]
+    args = [own, recv, table, up_table]
     specs = [
-        pl.BlockSpec(
-            (chans, cyls, 1, UP, 2 * FEEDS), lambda i, kk: (0, 0, pol, SUMS * kk[0] + block, 0)
-        ),
+        pl.BlockSpec((1, *own.shape[1:]), lambda i, kk: (index, 0, 0, 0, 0)),
         whole(recv),
         whole(table),
         whole(up_table),
@@ -153,10 +169,7 @@
         out = jax.ShapeDtypeStruct((FEEDS * CYLS, LANES), jnp.bfloat16)
     else:
         out = jax.ShapeDtypeStruct((CYLS, FEEDS, LANES), jnp.float32)
-    scratch = [pltpu.VMEM((CYLS * LANES, 2 * FEEDS), jnp.bfloat16)]
-    if last:
-        scratch.append(pltpu.VMEM((FEEDS * CYLS, LANES), jnp.float32))
-    flops = 2 * 512 * 512 * 512 + 2 * CYLS * 256 * 256 * 256
+    flops = 2 * 512 * 512 * 256 + 2 * CYLS * 256 * 256 * 256
     return pl.pallas_call(
         lambda *refs: step_kernel(first, last, *refs),
         out_shape=out,
@@ -165,7 +178,7 @@
             grid=(1,),
             in_specs=specs,
             out_specs=whole(out),
-            scratch_shapes=scratch,
+            scratch_shapes=[pltpu.VMEM((FEEDS * CYLS, LANES), jnp.float32)] if last else [],
         ),
         input_output_aliases=aliases,
         cost_estimate=pl.CostEstimate(flops=flops, bytes_accessed=2 << 20, transcendentals=0),
@@ -234,10 +247,12 @@
     pieces = split(source, which, steps[:1]) + split(source, which, steps[1:])
     received = [lax.ppermute(piece, "cyl", pair) for piece in pieces]
     others = lax.ppermute(gain_exponents, "cyl", pair)
+    own = own_partials(source, table, which)
     acc = None
-    for index, (pol, block) in enumerate(steps):
+    gains = (gain_exponents, others)
+    for index in range(len(steps)):
         first, last = index == 0, index == len(steps) - 1
-        acc = step(pol, block, first, last, which, volts, received[index], table, up_table, acc, (gain_exponents, others))
+        acc = step(index, first, last, which, own, received[index], table, up_table, acc, gains)
     sent = acc.reshape(256, 4, LANES)
     arrived = lax.all_to_all(sent, ("chan", "cyl"), split_axis=0, concat_axis=0, tiled=True)
     placed = place(arrived.reshape(1024, LANES))

time: 86.3 us -> 85.4 us (0.990)
  blocking collectives: 36.2 us -> 46.2 us
  waiting for transfers between devices: 19.7 us -> 10.1 us
  Pallas kernels: 11.4 us -> 10 us
    all_to_all x1, blocking collectives: 36.2 us -> 46.2 us  [local(): lax.all_to_all(sent, ('chan', 'cyl'), split_axis=0, concat_axis=0, tiled=...]
    ppermute x4, waiting for transfers between devices: 8.28 us -> 2.67 us  [local(): received = [lax.ppermute(piece, 'cyl', pair) for piece in pieces]]
    ppermute x1, waiting for transfers between devices: 11.4 us -> 7.45 us  [local(): others = lax.ppermute(gain_exponents, 'cyl', pair)]
    pallas_call x4, Pallas kernels: 7.42 us -> 3.55 us  [step(): pl.pallas_call(lambda *refs: step_kernel(first, last, *refs), out_shape=o...]
    pallas_call x0 -> x1, Pallas kernels: none -> 3.45 us  [own_partials(): pl.pallas_call(own_kernel, out_shape=jax.ShapeDtypeStruct(shape, jnp.bflo...]
    pallas_call x2, Pallas kernels: 3.12 us -> 2.15 us  [split(): pl.pallas_call(lambda *refs: split_kernel(steps, *refs), out_shape=[piece...]
  transfers between devices with their start and end apart: 5 -> 5, of which waited for: 3 -> 2; matrix products, arithmetic and copies ran while one was open for 0% -> 0% of each run, Pallas kernels for 9% -> 8%
where the time goes in v2:
time: 85.4 us; the launch traced here: 85.2 us
  blocking collectives  46.2 us (54%)
  starting transfers between devices  18.7 us (22%)
  waiting for transfers between devices  10.1 us (12%)
  Pallas kernels  10 us (12%)
    all_to_all x1, blocking collectives, local(): lax.all_to_all(sent, ('chan', 'cyl'), split_axis=0, concat_axis=0, tiled=...  46.2 us
    ppermute x4, starting transfers between devices, local(): received = [lax.ppermute(piece, 'cyl', pair) for piece in pieces]  13.4 us
    ppermute x1, waiting for transfers between devices, local(): others = lax.ppermute(gain_exponents, 'cyl', pair)  7.45 us
    ppermute x1, starting transfers between devices, local(): others = lax.ppermute(gain_exponents, 'cyl', pair)  5.29 us
    pallas_call x4, Pallas kernels, step(): pl.pallas_call(lambda *refs: step_kernel(first, last, *refs), out_shape=o...  3.55 us
    pallas_call x1, Pallas kernels, own_partials(): pl.pallas_call(own_kernel, out_shape=jax.ShapeDtypeStruct(shape, jnp.bflo...  3.45 us
    ppermute x4, waiting for transfers between devices, local(): received = [lax.ppermute(piece, 'cyl', pair) for piece in pieces]  2.67 us
    pallas_call x2, Pallas kernels, split(): pl.pallas_call(lambda *refs: split_kernel(steps, *refs), out_shape=[piece...  2.15 us
  transfers between devices with their start and end apart: 5, of which 2 were waited for; matrix products, arithmetic and copies ran while one was open for 0% of the time, Pallas kernels for 8%

profile of v2, /device:TPU:1, one launch (start us, length us, event | category | flops | bytes accessed | tf_op | source)
XLA Modules:
  0.0 85.2 jit_solution(12369883821828444872)
XLA Ops:
  0.0 0.0 copy-start.2
  0.0 1.0 %split.3 = bf16[8,2,16,512]{3,2,1,0:T(8,128)(2,1)S(1)} custom-call(s32[1]{0:T(128)} %bitcast.k_ref.refs_0_, bf16[8,2,2,64,512]{4,3,2,1,0:T(8,128)(2,1)} %refs_1_.3), custom_call_target="tpu_custom_call" | custom-call | tf_op jit(solution)/shard_map/split/pallas_call | solution.py:207
  1.0 7.8 %collective-permute-start.3 = (bf16[8,2,16,512]{3,2,1,0:T(8,128)(2,1)S(1)}, bf16[8,2,16,512]{3,2,1,0:T(8,128)(2,1)S(1)}, u32[]{:S(2)}, u32[]{:S(2)}) collective-permute-start(bf16[8,2,16,512]{3,2,1,0:T(8,128)(2,1)S(1)} %split.3), channel_id=1, source_target_pairs={{0,1},{1,0},{2,3},{3,2},{4,5},{5,4},{6,7},{7,6},{8,9},{9,8},{10,11... | collective-permute-start | bytes 786440 | tf_op jit(solution)/shard_map/ppermute | solution.py:248
  8.9 1.1 %split.2 = (bf16[8,2,16,512]{3,2,1,0:T(8,128)(2,1)S(1)}, bf16[8,2,16,512]{3,2,1,0:T(8,128)(2,1)S(1)}, bf16[8,2,16,512]{3,2,1,0:T(8,128)(2,1)S(1)}) custom-call(s32[1]{0:T(128)} %bitcast.k_ref.refs_0_, bf16[8,2,2,64,512]{4,3,2,1,0:T(8,128)(2,1)} %refs_1_.3), custom_call_target="tpu_custom_call" | custom-call | tf_op jit(solution)/shard_map/split/pallas_call | solution.py:207
  10.0 0.1 collective-permute-start.2
  10.1 5.4 %collective-permute-start.1 = (bf16[8,2,16,512]{3,2,1,0:T(8,128)(2,1)S(1)}, bf16[8,2,16,512]{3,2,1,0:T(8,128)(2,1)S(1)}, u32[]{:S(2)}, u32[]{:S(2)}) collective-permute-start(bf16[8,2,16,512]{3,2,1,0:T(8,128)(2,1)S(1)} %get-tuple-element.9), channel_id=1, source_target_pairs={{0,1},{1,0},{2,3},{3,2},{4,5},{5,4},{6,7},{7,6},{8,9},{9,8},{10,11... | collective-permute-start | bytes 786440 | tf_op jit(solution)/shard_map/ppermute | solution.py:248
  15.5 0.1 collective-permute-start
  15.6 0.0 copy-done.2
  15.6 0.1 copy.8.refs_6_
  15.6 5.3 %collective-permute-start.4 = (s32[8,2]{1,0:T(8,128)S(1)}, s32[8,2]{1,0:T(8,128)S(1)}, u32[]{:S(2)}, u32[]{:S(2)}) collective-permute-start(s32[8,2]{1,0:T(8,128)S(1)} %copy.8.refs_6_), channel_id=1, source_target_pairs={{0,1},{1,0},{2,3},{3,2},{4,5},{5,4},{6,7},{7,6},{8,9},{9,8},{10,11... | collective-permute-start | bytes 200 | tf_op jit(solution)/shard_map/ppermute | solution.py:249
  20.9 0.0 copy-done
  20.9 3.5 %own_partials.1.refs_1_ = bf16[4,4,2,256,128]{4,3,2,1,0:T(8,128)(2,1)S(1)} custom-call(s32[1]{0:T(128)} %bitcast.k_ref.refs_0_, bf16[8,2,2,64,512]{4,3,2,1,0:T(8,128)(2,1)} %refs_1_.3, bf16[512,512]{1,0:T(8,128)(2,1)S(1)} %copy-done), custom_call_target="tpu_custom_call" | custom-call | flops 536870912 | bytes 4194304 | tf_op jit(solution)/shard_map/own_partials/pallas_call | solution.py:93
  24.4 0.0 collective-permute-done.3.refs_2_
  24.4 0.0 copy-done.1
  24.4 0.9 %beam_step.3.refs_5_ = f32[4,256,128]{2,1,0:T(8,128)S(1)} custom-call(s32[1]{0:T(128)} %bitcast.k_ref.refs_0_, bf16[4,4,2,256,128]{4,3,2,1,0:T(8,128)(2,1)S(1)} %own_partials.1.refs_1_, bf16[8,2,16,512]{3,2,1,0:T(8,128)(2,1)S(1)} %collective-permute-done.3.refs_2_, bf16[512,512]{1,0:T(8,128)(2,1)S(1)} %copy-done, bf16[256,256]{1,0:T(8,128)(2,1)S(1)} %copy-done.1), custom_call_target="tpu_custom_call" | custom-call | flops 268435456 | bytes 2097152 | tf_op jit(solution)/shard_map/beam_step/pallas_call | solution.py:173
  25.3 0.0 collective-permute-done.2.refs_2_
  25.3 0.9 %beam_step.4.refs_5_ = f32[4,256,128]{2,1,0:T(8,128)S(1)} custom-call(s32[1]{0:T(128)} %bitcast.k_ref.refs_0_, bf16[4,4,2,256,128]{4,3,2,1,0:T(8,128)(2,1)S(1)} %own_partials.1.refs_1_, bf16[8,2,16,512]{3,2,1,0:T(8,128)(2,1)S(1)} %collective-permute-done.2.refs_2_, bf16[512,512]{1,0:T(8,128)(2,1)S(1)} %copy-done, ...), custom_call_target="tpu_custom_call", output_to_operand_aliasing={{}: (5, {})} | custom-call | flops 268435456 | bytes 2097152 | tf_op jit(solution)/shard_map/beam_step/pallas_call | solution.py:173
  26.2 2.7 %collective-permute-done.1.refs_2_ = bf16[8,2,16,512]{3,2,1,0:T(8,128)(2,1)S(1)} collective-permute-done((bf16[8,2,16,512]{3,2,1,0:T(8,128)(2,1)S(1)}, bf16[8,2,16,512]{3,2,1,0:T(8,128)(2,1)S(1)}, u32[]{:S(2)}, u32[]{:S(2)}) %collective-permute-start.1) | collective-permute-done | bytes 262176 | tf_op jit(solution)/shard_map/ppermute | solution.py:248
  28.9 0.9 %beam_step.5.refs_5_ = f32[4,256,128]{2,1,0:T(8,128)S(1)} custom-call(s32[1]{0:T(128)} %bitcast.k_ref.refs_0_, bf16[4,4,2,256,128]{4,3,2,1,0:T(8,128)(2,1)S(1)} %own_partials.1.refs_1_, bf16[8,2,16,512]{3,2,1,0:T(8,128)(2,1)S(1)} %collective-permute-done.1.refs_2_, bf16[512,512]{1,0:T(8,128)(2,1)S(1)} %copy-done, ...), custom_call_target="tpu_custom_call", output_to_operand_aliasing={{}: (5, {})} | custom-call | flops 268435456 | bytes 2097152 | tf_op jit(solution)/shard_map/beam_step/pallas_call | solution.py:173
  29.8 7.4 %collective-permute-done.4.refs_7_ = s32[8,2]{1,0:T(8,128)S(1)} collective-permute-done((s32[8,2]{1,0:T(8,128)S(1)}, s32[8,2]{1,0:T(8,128)S(1)}, u32[]{:S(2)}, u32[]{:S(2)}) %collective-permute-start.4) | collective-permute-done | bytes 96 | tf_op jit(solution)/shard_map/ppermute | solution.py:249
  37.2 0.0 collective-permute-done.refs_2_
  37.2 0.9 %beam_step_last.1 = bf16[1024,128]{1,0:T(8,128)(2,1)S(1)} custom-call(s32[1]{0:T(128)} %bitcast.k_ref.refs_0_, bf16[4,4,2,256,128]{4,3,2,1,0:T(8,128)(2,1)S(1)} %own_partials.1.refs_1_, bf16[8,2,16,512]{3,2,1,0:T(8,128)(2,1)S(1)} %collective-permute-done.refs_2_, bf16[512,512]{1,0:T(8,128)(2,1)S(1)} %copy-done, bf16[256,256]{1,0:T(8,128)(2,1)S(1)} %copy-done.1, ...), custom_call_target="tpu_custom_call" | custom-call | flops 268435456 | bytes 2097152 | tf_op jit(solution)/shard_map/beam_step_last/pallas_call | solution.py:173
  38.1 46.2 %all_to_all.5 = bf16[256,4,128]{2,1,0:T(4,128)(2,1)S(1)} all-to-all(bf16[256,4,128]{2,1,0:T(4,128)(2,1)S(1)} %bitcast.8), channel_id=1, replica_groups=mesh['chan'=128,'cyl'=2] {'chan','cyl'}, dimensions={0} | all-to-all | bytes 524288 | tf_op jit(solution)/shard_map/all_to_all | solution.py:257
  84.4 0.9 %place.1 = f32[4,256,128]{2,1,0:T(8,128)} custom-call(bf16[1024,128]{1,0:T(8,128)(2,1)S(1)} %bitcast.9), custom_call_target="tpu_custom_call" | custom-call | tf_op jit(solution)/shard_map/place/pallas_call | solution.py:229
  (2 shorter events, 0.0 us)
Async XLA Ops:
  0.0 15.6 %copy-start.2 = (s32[8,2]{0,1:T(2,128)S(1)}, s32[8,2]{0,1:T(2,128)}, u32[]{:S(2)}) copy-start(s32[8,2]{0,1:T(2,128)} %param.5) | copy-start | bytes 196
  0.0 20.9 %copy-start = (bf16[512,512]{1,0:T(8,128)(2,1)S(1)}, bf16[512,512]{1,0:T(8,128)(2,1)}, u32[]{:S(2)}) copy-start(bf16[512,512]{1,0:T(8,128)(2,1)} %constant.8.clone.t_ref.refs_3_) | copy-start | bytes 1572868
  1.0 23.4 %collective-permute-start.3 = (bf16[8,2,16,512]{3,2,1,0:T(8,128)(2,1)S(1)}, bf16[8,2,16,512]{3,2,1,0:T(8,128)(2,1)S(1)}, u32[]{:S(2)}, u32[]{:S(2)}) collective-permute-start(bf16[8,2,16,512]{3,2,1,0:T(8,128)(2,1)S(1)} %split.3), channel_id=1, source_target_pairs={{0,1},{1,0},{2,3},{3,2},{4,5},{5,4},{6,7},{7,6},{8,9},{9,8},{10,11... | collective-permute-start | bytes 786440 | tf_op jit(solution)/shard_map/ppermute | solution.py:248
  10.0 15.3 %collective-permute-start.2 = (bf16[8,2,16,512]{3,2,1,0:T(8,128)(2,1)S(1)}, bf16[8,2,16,512]{3,2,1,0:T(8,128)(2,1)S(1)}, u32[]{:S(2)}, u32[]{:S(2)}) collective-permute-start(bf16[8,2,16,512]{3,2,1,0:T(8,128)(2,1)S(1)} %get-tuple-element.10), channel_id=1, source_target_pairs={{0,1},{1,0},{2,3},{3,2},{4,5},{5,4},{6,7},{7,6},{8,9},{9,8},{10,11... | collective-permute-start | bytes 786440 | tf_op jit(solution)/shard_map/ppermute | solution.py:248
  10.1 18.8 %collective-permute-start.1 = (bf16[8,2,16,512]{3,2,1,0:T(8,128)(2,1)S(1)}, bf16[8,2,16,512]{3,2,1,0:T(8,128)(2,1)S(1)}, u32[]{:S(2)}, u32[]{:S(2)}) collective-permute-start(bf16[8,2,16,512]{3,2,1,0:T(8,128)(2,1)S(1)} %get-tuple-element.9), channel_id=1, source_target_pairs={{0,1},{1,0},{2,3},{3,2},{4,5},{5,4},{6,7},{7,6},{8,9},{9,8},{10,11... | collective-permute-start | bytes 786440 | tf_op jit(solution)/shard_map/ppermute | solution.py:248
  15.5 21.8 %collective-permute-start = (bf16[8,2,16,512]{3,2,1,0:T(8,128)(2,1)S(1)}, bf16[8,2,16,512]{3,2,1,0:T(8,128)(2,1)S(1)}, u32[]{:S(2)}, u32[]{:S(2)}) collective-permute-start(bf16[8,2,16,512]{3,2,1,0:T(8,128)(2,1)S(1)} %get-tuple-element.8), channel_id=1, source_target_pairs={{0,1},{1,0},{2,3},{3,2},{4,5},{5,4},{6,7},{7,6},{8,9},{9,8},{10,11... | collective-permute-start | bytes 786440 | tf_op jit(solution)/shard_map/ppermute | solution.py:248
  15.6 8.8 %copy-start.1 = (bf16[256,256]{1,0:T(8,128)(2,1)S(1)}, bf16[256,256]{1,0:T(8,128)(2,1)}, u32[]{:S(2)}) copy-start(bf16[256,256]{1,0:T(8,128)(2,1)} %constant.9.clone.refs_4_) | copy-start | bytes 393220
  15.6 21.6 %collective-permute-start.4 = (s32[8,2]{1,0:T(8,128)S(1)}, s32[8,2]{1,0:T(8,128)S(1)}, u32[]{:S(2)}, u32[]{:S(2)}) collective-permute-start(s32[8,2]{1,0:T(8,128)S(1)} %copy.8.refs_6_), channel_id=1, source_target_pairs={{0,1},{1,0},{2,3},{3,2},{4,5},{5,4},{6,7},{7,6},{8,9},{9,8},{10,11... | collective-permute-start | bytes 200 | tf_op jit(solution)/shard_map/ppermute | solution.py:249

commit v3 on v2

--- a/solution.py
+++ b/solution.py
@@ -128,14 +128,12 @@
     for low in range(2):
         rows = pl.ds(low * half, half)
         for e, (other_r, other_i) in enumerate(ns_partials(x, t_ref, low, sign)):
-            own_r = own_ref[0, e, 0, rows, :].astype(jnp.float32)
-            own_i = own_ref[0, e, 1, rows, :].astype(jnp.float32)
-            other_r, other_i = other_r.astype(jnp.float32), other_i.astype(jnp.float32)
+            own_r, own_i = own_ref[0, e, 0, rows, :], own_ref[0, e, 1, rows, :]
             if e % 2 == 0:
                 coded = own_r + other_i, own_i - other_r
             else:
                 coded = own_r - other_i, own_i + other_r
-            both = jnp.concatenate([part.astype(jnp.bfloat16) for part in coded], axis=1)
+            both = jnp.concatenate(coded, axis=1)
             spectra = jnp.dot(both, u_ref[...], preferred_element_type=jnp.float32)
             squared = spectra * spectra
             power = squared[:, :LANES] + squared[:, LANES:]

time: 85.4 us -> 85.4 us (level)
  no operation moved by 1% of the time
where the time goes in v3:
time: 85.4 us; the launch traced here: 85.2 us
  blocking collectives  46.2 us (54%)
  starting transfers between devices  18.7 us (22%)
  waiting for transfers between devices  10.1 us (12%)
  Pallas kernels  9.97 us (12%)
    all_to_all x1, blocking collectives, local(): lax.all_to_all(sent, ('chan', 'cyl'), split_axis=0, concat_axis=0, tiled=...  46.2 us
    ppermute x4, starting transfers between devices, local(): received = [lax.ppermute(piece, 'cyl', pair) for piece in pieces]  13.4 us
    ppermute x1, waiting for transfers between devices, local(): others = lax.ppermute(gain_exponents, 'cyl', pair)  7.45 us
    ppermute x1, starting transfers between devices, local(): others = lax.ppermute(gain_exponents, 'cyl', pair)  5.29 us
    pallas_call x4, Pallas kernels, step(): pl.pallas_call(lambda *refs: step_kernel(first, last, *refs), out_shape=o...  3.5 us
    pallas_call x1, Pallas kernels, own_partials(): pl.pallas_call(own_kernel, out_shape=jax.ShapeDtypeStruct(shape, jnp.bflo...  3.45 us
    ppermute x4, waiting for transfers between devices, local(): received = [lax.ppermute(piece, 'cyl', pair) for piece in pieces]  2.7 us
    pallas_call x2, Pallas kernels, split(): pl.pallas_call(lambda *refs: split_kernel(steps, *refs), out_shape=[piece...  2.15 us
  transfers between devices with their start and end apart: 5, of which 2 were waited for; matrix products, arithmetic and copies ran while one was open for 0% of the time, Pallas kernels for 8%

profile of v3, /device:TPU:1, one launch (start us, length us, event | category | flops | bytes accessed | tf_op | source)
XLA Modules:
  0.0 85.2 jit_solution(7894394654950448731)
XLA Ops:
  0.0 0.0 copy-start.2
  0.0 1.0 %split.3 = bf16[8,2,16,512]{3,2,1,0:T(8,128)(2,1)S(1)} custom-call(s32[1]{0:T(128)} %bitcast.k_ref.refs_0_, bf16[8,2,2,64,512]{4,3,2,1,0:T(8,128)(2,1)} %refs_1_.3), custom_call_target="tpu_custom_call" | custom-call | tf_op jit(solution)/shard_map/split/pallas_call | solution.py:205
  1.0 7.8 %collective-permute-start.3 = (bf16[8,2,16,512]{3,2,1,0:T(8,128)(2,1)S(1)}, bf16[8,2,16,512]{3,2,1,0:T(8,128)(2,1)S(1)}, u32[]{:S(2)}, u32[]{:S(2)}) collective-permute-start(bf16[8,2,16,512]{3,2,1,0:T(8,128)(2,1)S(1)} %split.3), channel_id=1, source_target_pairs={{0,1},{1,0},{2,3},{3,2},{4,5},{5,4},{6,7},{7,6},{8,9},{9,8},{10,11... | collective-permute-start | bytes 786440 | tf_op jit(solution)/shard_map/ppermute | solution.py:246
  8.9 1.1 %split.2 = (bf16[8,2,16,512]{3,2,1,0:T(8,128)(2,1)S(1)}, bf16[8,2,16,512]{3,2,1,0:T(8,128)(2,1)S(1)}, bf16[8,2,16,512]{3,2,1,0:T(8,128)(2,1)S(1)}) custom-call(s32[1]{0:T(128)} %bitcast.k_ref.refs_0_, bf16[8,2,2,64,512]{4,3,2,1,0:T(8,128)(2,1)} %refs_1_.3), custom_call_target="tpu_custom_call" | custom-call | tf_op jit(solution)/shard_map/split/pallas_call | solution.py:205
  10.0 0.1 collective-permute-start.2
  10.1 5.4 %collective-permute-start.1 = (bf16[8,2,16,512]{3,2,1,0:T(8,128)(2,1)S(1)}, bf16[8,2,16,512]{3,2,1,0:T(8,128)(2,1)S(1)}, u32[]{:S(2)}, u32[]{:S(2)}) collective-permute-start(bf16[8,2,16,512]{3,2,1,0:T(8,128)(2,1)S(1)} %get-tuple-element.9), channel_id=1, source_target_pairs={{0,1},{1,0},{2,3},{3,2},{4,5},{5,4},{6,7},{7,6},{8,9},{9,8},{10,11... | collective-permute-start | bytes 786440 | tf_op jit(solution)/shard_map/ppermute | solution.py:246
  15.5 0.1 collective-permute-start
  15.6 0.0 copy-done.2
  15.6 0.1 copy.8.refs_6_
  15.6 5.3 %collective-permute-start.4 = (s32[8,2]{1,0:T(8,128)S(1)}, s32[8,2]{1,0:T(8,128)S(1)}, u32[]{:S(2)}, u32[]{:S(2)}) collective-permute-start(s32[8,2]{1,0:T(8,128)S(1)} %copy.8.refs_6_), channel_id=1, source_target_pairs={{0,1},{1,0},{2,3},{3,2},{4,5},{5,4},{6,7},{7,6},{8,9},{9,8},{10,11... | collective-permute-start | bytes 200 | tf_op jit(solution)/shard_map/ppermute | solution.py:247
  20.9 0.0 copy-done
  20.9 3.5 %own_partials.1.refs_1_ = bf16[4,4,2,256,128]{4,3,2,1,0:T(8,128)(2,1)S(1)} custom-call(s32[1]{0:T(128)} %bitcast.k_ref.refs_0_, bf16[8,2,2,64,512]{4,3,2,1,0:T(8,128)(2,1)} %refs_1_.3, bf16[512,512]{1,0:T(8,128)(2,1)S(1)} %copy-done), custom_call_target="tpu_custom_call" | custom-call | flops 536870912 | bytes 4194304 | tf_op jit(solution)/shard_map/own_partials/pallas_call | solution.py:93
  24.4 0.0 collective-permute-done.3.refs_2_
  24.4 0.0 copy-done.1
  24.4 0.9 %beam_step.3.refs_5_ = f32[4,256,128]{2,1,0:T(8,128)S(1)} custom-call(s32[1]{0:T(128)} %bitcast.k_ref.refs_0_, bf16[4,4,2,256,128]{4,3,2,1,0:T(8,128)(2,1)S(1)} %own_partials.1.refs_1_, bf16[8,2,16,512]{3,2,1,0:T(8,128)(2,1)S(1)} %collective-permute-done.3.refs_2_, bf16[512,512]{1,0:T(8,128)(2,1)S(1)} %copy-done, bf16[256,256]{1,0:T(8,128)(2,1)S(1)} %copy-done.1), custom_call_target="tpu_custom_call" | custom-call | flops 268435456 | bytes 2097152 | tf_op jit(solution)/shard_map/beam_step/pallas_call | solution.py:171
  25.3 0.0 collective-permute-done.2.refs_2_
  25.3 0.9 %beam_step.4.refs_5_ = f32[4,256,128]{2,1,0:T(8,128)S(1)} custom-call(s32[1]{0:T(128)} %bitcast.k_ref.refs_0_, bf16[4,4,2,256,128]{4,3,2,1,0:T(8,128)(2,1)S(1)} %own_partials.1.refs_1_, bf16[8,2,16,512]{3,2,1,0:T(8,128)(2,1)S(1)} %collective-permute-done.2.refs_2_, bf16[512,512]{1,0:T(8,128)(2,1)S(1)} %copy-done, ...), custom_call_target="tpu_custom_call", output_to_operand_aliasing={{}: (5, {})} | custom-call | flops 268435456 | bytes 2097152 | tf_op jit(solution)/shard_map/beam_step/pallas_call | solution.py:171
  26.2 2.7 %collective-permute-done.1.refs_2_ = bf16[8,2,16,512]{3,2,1,0:T(8,128)(2,1)S(1)} collective-permute-done((bf16[8,2,16,512]{3,2,1,0:T(8,128)(2,1)S(1)}, bf16[8,2,16,512]{3,2,1,0:T(8,128)(2,1)S(1)}, u32[]{:S(2)}, u32[]{:S(2)}) %collective-permute-start.1) | collective-permute-done | bytes 262176 | tf_op jit(solution)/shard_map/ppermute | solution.py:246
  28.9 0.9 %beam_step.5.refs_5_ = f32[4,256,128]{2,1,0:T(8,128)S(1)} custom-call(s32[1]{0:T(128)} %bitcast.k_ref.refs_0_, bf16[4,4,2,256,128]{4,3,2,1,0:T(8,128)(2,1)S(1)} %own_partials.1.refs_1_, bf16[8,2,16,512]{3,2,1,0:T(8,128)(2,1)S(1)} %collective-permute-done.1.refs_2_, bf16[512,512]{1,0:T(8,128)(2,1)S(1)} %copy-done, ...), custom_call_target="tpu_custom_call", output_to_operand_aliasing={{}: (5, {})} | custom-call | flops 268435456 | bytes 2097152 | tf_op jit(solution)/shard_map/beam_step/pallas_call | solution.py:171
  29.8 7.4 %collective-permute-done.4.refs_7_ = s32[8,2]{1,0:T(8,128)S(1)} collective-permute-done((s32[8,2]{1,0:T(8,128)S(1)}, s32[8,2]{1,0:T(8,128)S(1)}, u32[]{:S(2)}, u32[]{:S(2)}) %collective-permute-start.4) | collective-permute-done | bytes 96 | tf_op jit(solution)/shard_map/ppermute | solution.py:247
  37.2 0.0 collective-permute-done.refs_2_
  37.2 0.9 %beam_step_last.1 = bf16[1024,128]{1,0:T(8,128)(2,1)S(1)} custom-call(s32[1]{0:T(128)} %bitcast.k_ref.refs_0_, bf16[4,4,2,256,128]{4,3,2,1,0:T(8,128)(2,1)S(1)} %own_partials.1.refs_1_, bf16[8,2,16,512]{3,2,1,0:T(8,128)(2,1)S(1)} %collective-permute-done.refs_2_, bf16[512,512]{1,0:T(8,128)(2,1)S(1)} %copy-done, bf16[256,256]{1,0:T(8,128)(2,1)S(1)} %copy-done.1, ...), custom_call_target="tpu_custom_call" | custom-call | flops 268435456 | bytes 2097152 | tf_op jit(solution)/shard_map/beam_step_last/pallas_call | solution.py:171
  38.1 46.2 %all_to_all.5 = bf16[256,4,128]{2,1,0:T(4,128)(2,1)S(1)} all-to-all(bf16[256,4,128]{2,1,0:T(4,128)(2,1)S(1)} %bitcast.8), channel_id=1, replica_groups=mesh['chan'=128,'cyl'=2] {'chan','cyl'}, dimensions={0} | all-to-all | bytes 524288 | tf_op jit(solution)/shard_map/all_to_all | solution.py:255
  84.3 0.9 %place.1 = f32[4,256,128]{2,1,0:T(8,128)} custom-call(bf16[1024,128]{1,0:T(8,128)(2,1)S(1)} %bitcast.9), custom_call_target="tpu_custom_call" | custom-call | tf_op jit(solution)/shard_map/place/pallas_call | solution.py:227
  (2 shorter events, 0.0 us)
Async XLA Ops:
  0.0 15.6 %copy-start.2 = (s32[8,2]{0,1:T(2,128)S(1)}, s32[8,2]{0,1:T(2,128)}, u32[]{:S(2)}) copy-start(s32[8,2]{0,1:T(2,128)} %param.5) | copy-start | bytes 196
  0.0 20.9 %copy-start = (bf16[512,512]{1,0:T(8,128)(2,1)S(1)}, bf16[512,512]{1,0:T(8,128)(2,1)}, u32[]{:S(2)}) copy-start(bf16[512,512]{1,0:T(8,128)(2,1)} %constant.8.clone.t_ref.refs_3_) | copy-start | bytes 1572868
  1.0 23.4 %collective-permute-start.3 = (bf16[8,2,16,512]{3,2,1,0:T(8,128)(2,1)S(1)}, bf16[8,2,16,512]{3,2,1,0:T(8,128)(2,1)S(1)}, u32[]{:S(2)}, u32[]{:S(2)}) collective-permute-start(bf16[8,2,16,512]{3,2,1,0:T(8,128)(2,1)S(1)} %split.3), channel_id=1, source_target_pairs={{0,1},{1,0},{2,3},{3,2},{4,5},{5,4},{6,7},{7,6},{8,9},{9,8},{10,11... | collective-permute-start | bytes 786440 | tf_op jit(solution)/shard_map/ppermute | solution.py:246
  10.0 15.3 %collective-permute-start.2 = (bf16[8,2,16,512]{3,2,1,0:T(8,128)(2,1)S(1)}, bf16[8,2,16,512]{3,2,1,0:T(8,128)(2,1)S(1)}, u32[]{:S(2)}, u32[]{:S(2)}) collective-permute-start(bf16[8,2,16,512]{3,2,1,0:T(8,128)(2,1)S(1)} %get-tuple-element.10), channel_id=1, source_target_pairs={{0,1},{1,0},{2,3},{3,2},{4,5},{5,4},{6,7},{7,6},{8,9},{9,8},{10,11... | collective-permute-start | bytes 786440 | tf_op jit(solution)/shard_map/ppermute | solution.py:246
  10.1 18.8 %collective-permute-start.1 = (bf16[8,2,16,512]{3,2,1,0:T(8,128)(2,1)S(1)}, bf16[8,2,16,512]{3,2,1,0:T(8,128)(2,1)S(1)}, u32[]{:S(2)}, u32[]{:S(2)}) collective-permute-start(bf16[8,2,16,512]{3,2,1,0:T(8,128)(2,1)S(1)} %get-tuple-element.9), channel_id=1, source_target_pairs={{0,1},{1,0},{2,3},{3,2},{4,5},{5,4},{6,7},{7,6},{8,9},{9,8},{10,11... | collective-permute-start | bytes 786440 | tf_op jit(solution)/shard_map/ppermute | solution.py:246
  15.5 21.8 %collective-permute-start = (bf16[8,2,16,512]{3,2,1,0:T(8,128)(2,1)S(1)}, bf16[8,2,16,512]{3,2,1,0:T(8,128)(2,1)S(1)}, u32[]{:S(2)}, u32[]{:S(2)}) collective-permute-start(bf16[8,2,16,512]{3,2,1,0:T(8,128)(2,1)S(1)} %get-tuple-element.8), channel_id=1, source_target_pairs={{0,1},{1,0},{2,3},{3,2},{4,5},{5,4},{6,7},{7,6},{8,9},{9,8},{10,11... | collective-permute-start | bytes 786440 | tf_op jit(solution)/shard_map/ppermute | solution.py:246
  15.6 8.8 %copy-start.1 = (bf16[256,256]{1,0:T(8,128)(2,1)S(1)}, bf16[256,256]{1,0:T(8,128)(2,1)}, u32[]{:S(2)}) copy-start(bf16[256,256]{1,0:T(8,128)(2,1)} %constant.9.clone.refs_4_) | copy-start | bytes 393220
  15.6 21.6 %collective-permute-start.4 = (s32[8,2]{1,0:T(8,128)S(1)}, s32[8,2]{1,0:T(8,128)S(1)}, u32[]{:S(2)}, u32[]{:S(2)}) collective-permute-start(s32[8,2]{1,0:T(8,128)S(1)} %copy.8.refs_6_), channel_id=1, source_target_pairs={{0,1},{1,0},{2,3},{3,2},{4,5},{5,4},{6,7},{7,6},{8,9},{9,8},{10,11... | collective-permute-start | bytes 200 | tf_op jit(solution)/shard_map/ppermute | solution.py:247

commit v4 on v3

--- a/solution.py
+++ b/solution.py
@@ -49,8 +49,8 @@
     return [(r.astype(jnp.bfloat16), i.astype(jnp.bfloat16)) for r, i in beams]
 
 
-def ns_partials(x, t_ref, low, sign):
-    dims = (((1,), (1,)), ((), ()))
+def ns_partials(x, t_ref, low, sign, turned=False):
+    dims = (((1,), (0 if turned else 1,)), ((), ()))
     half = FEEDS // 2
     real = lax.dot_general(t_ref[pl.ds(low * half, half), :], x, dims, preferred_element_type=jnp.float32)
     imag = lax.dot_general(t_ref[pl.ds(FEEDS + low * half, half), :], x, dims, preferred_element_type=jnp.float32)
@@ -123,11 +123,11 @@
     if last:
         scale = gain_rows(k, *gain_refs)
     sign = (1 - 2 * k).astype(jnp.float32)
-    x = pair_rows(lambda cyl: recv_ref[:, cyl])
+    x = recv_ref[...] if last else pair_rows(lambda cyl: recv_ref[:, cyl])
     half = FEEDS // 2
     for low in range(2):
         rows = pl.ds(low * half, half)
-        for e, (other_r, other_i) in enumerate(ns_partials(x, t_ref, low, sign)):
+        for e, (other_r, other_i) in enumerate(ns_partials(x, t_ref, low, sign, last)):
             own_r, own_i = own_ref[0, e, 0, rows, :], own_ref[0, e, 1, rows, :]
             if e % 2 == 0:
                 coded = own_r + other_i, own_i - other_r
@@ -217,6 +217,31 @@
     )(which, volts)
 
 
+def turn_kernel(k_ref, volts_ref, out_ref):
+    out_ref[...] = pair_rows(lambda cyl: volts_ref[:, cyl, 0]).T
+
+
+def turned_piece(volts, which, pol, block):
+    chans, cyls = volts.shape[:2]
+    return pl.pallas_call(
+        turn_kernel,
+        out_shape=jax.ShapeDtypeStruct((2 * FEEDS, 2 * LANES), volts.dtype),
+        grid_spec=pltpu.PrefetchScalarGridSpec(
+            num_scalar_prefetch=1,
+            grid=(1,),
+            in_specs=[
+                pl.BlockSpec(
+                    (chans, cyls, 1, UP, 2 * FEEDS),
+                    lambda i, kk: (0, 0, pol, SUMS * (1 - kk[0]) + block, 0),
+                )
+            ],
+            out_specs=pl.BlockSpec((2 * FEEDS, 2 * LANES), lambda i, kk: (0, 0)),
+        ),
+        compiler_params=pltpu.CompilerParams(vmem_limit_bytes=8 << 20),
+        name="turned_piece",
+    )(which, volts)
+
+
 def place_kernel(in_ref, out_ref, wide_ref):
     wide_ref[...] = in_ref[...].astype(jnp.float32)
     for row in range(4):
@@ -242,7 +267,11 @@
     steps = [(pol, block) for pol in range(POLS) for block in range(SUMS)]
     which = k.astype(jnp.int32).reshape(1)
     source = pltpu.with_memory_space_constraint(volts, pltpu.HBM)
-    pieces = split(source, which, steps[:1]) + split(source, which, steps[1:])
+    pieces = [
+        *split(source, which, steps[:1]),
+        *split(source, which, steps[1:-1]),
+        turned_piece(source, which, *steps[-1]),
+    ]
     received = [lax.ppermute(piece, "cyl", pair) for piece in pieces]
     others = lax.ppermute(gain_exponents, "cyl", pair)
     own = own_partials(source, table, which)

time: 85.4 us -> 85.2 us (level)
  waiting for transfers between devices: 10.1 us -> 9.17 us
    pallas_call x0 -> x1, Pallas kernels: none -> 1.07 us  [turned_piece(): pl.pallas_call(turn_kernel, out_shape=jax.ShapeDtypeStruct((2 * FEEDS, 2...]
    ppermute x4, waiting for transfers between devices: 2.7 us -> 1.72 us  [local(): received = [lax.ppermute(piece, 'cyl', pair) for piece in pieces]]
  transfers between devices with their start and end apart: 5 -> 5, of which waited for: 2 -> 2; matrix products, arithmetic and copies ran while one was open for 0% -> 0% of each run, Pallas kernels for 8% -> 10%
where the time goes in v4:
time: 85.2 us; the launch traced here: 85 us
  blocking collectives  46.2 us (54%)
  starting transfers between devices  18.8 us (22%)
  Pallas kernels  10.7 us (13%)
  waiting for transfers between devices  9.17 us (11%)
    all_to_all x1, blocking collectives, local(): lax.all_to_all(sent, ('chan', 'cyl'), split_axis=0, concat_axis=0, tiled=...  46.2 us
    ppermute x4, starting transfers between devices, local(): received = [lax.ppermute(piece, 'cyl', pair) for piece in pieces]  13.5 us
    ppermute x1, waiting for transfers between devices, local(): others = lax.ppermute(gain_exponents, 'cyl', pair)  7.45 us
    ppermute x1, starting transfers between devices, local(): others = lax.ppermute(gain_exponents, 'cyl', pair)  5.29 us
    pallas_call x1, Pallas kernels, own_partials(): pl.pallas_call(own_kernel, out_shape=jax.ShapeDtypeStruct(shape, jnp.bflo...  3.46 us
    pallas_call x4, Pallas kernels, step(): pl.pallas_call(lambda *refs: step_kernel(first, last, *refs), out_shape=o...  3.33 us
    pallas_call x2, Pallas kernels, split(): pl.pallas_call(lambda *refs: split_kernel(steps, *refs), out_shape=[piece...  2 us
    ppermute x4, waiting for transfers between devices, local(): received = [lax.ppermute(piece, 'cyl', pair) for piece in pieces]  1.72 us
  transfers between devices with their start and end apart: 5, of which 2 were waited for; matrix products, arithmetic and copies ran while one was open for 0% of the time, Pallas kernels for 10%

profile of v4, /device:TPU:1, one launch (start us, length us, event | category | flops | bytes accessed | tf_op | source)
XLA Modules:
  0.0 85.0 jit_solution(11465969688711305270)
XLA Ops:
  0.0 1.0 %split.3 = bf16[8,2,16,512]{3,2,1,0:T(8,128)(2,1)S(1)} custom-call(s32[1]{0:T(128)} %bitcast.k_ref.refs_0_, bf16[8,2,2,64,512]{4,3,2,1,0:T(8,128)(2,1)} %refs_1_.3), custom_call_target="tpu_custom_call" | custom-call | tf_op jit(solution)/shard_map/split/pallas_call | solution.py:205
  1.0 0.0 copy-start.2
  1.0 0.0 copy-start
  1.0 7.8 %collective-permute-start.3 = (bf16[8,2,16,512]{3,2,1,0:T(8,128)(2,1)S(1)}, bf16[8,2,16,512]{3,2,1,0:T(8,128)(2,1)S(1)}, u32[]{:S(2)}, u32[]{:S(2)}) collective-permute-start(bf16[8,2,16,512]{3,2,1,0:T(8,128)(2,1)S(1)} %split.3), channel_id=1, source_target_pairs={{0,1},{1,0},{2,3},{3,2},{4,5},{5,4},{6,7},{7,6},{8,9},{9,8},{10,11... | collective-permute-start | bytes 786440 | tf_op jit(solution)/shard_map/ppermute | solution.py:275
  8.8 1.0 %split.2 = (bf16[8,2,16,512]{3,2,1,0:T(8,128)(2,1)S(1)}, bf16[8,2,16,512]{3,2,1,0:T(8,128)(2,1)S(1)}) custom-call(s32[1]{0:T(128)} %bitcast.k_ref.refs_0_, bf16[8,2,2,64,512]{4,3,2,1,0:T(8,128)(2,1)} %refs_1_.3), custom_call_target="tpu_custom_call" | custom-call | tf_op jit(solution)/shard_map/split/pallas_call | solution.py:205
  9.9 0.2 collective-permute-start.2
  10.0 5.3 %collective-permute-start.1 = (bf16[8,2,16,512]{3,2,1,0:T(8,128)(2,1)S(1)}, bf16[8,2,16,512]{3,2,1,0:T(8,128)(2,1)S(1)}, u32[]{:S(2)}, u32[]{:S(2)}) collective-permute-start(bf16[8,2,16,512]{3,2,1,0:T(8,128)(2,1)S(1)} %get-tuple-element.7), channel_id=1, source_target_pairs={{0,1},{1,0},{2,3},{3,2},{4,5},{5,4},{6,7},{7,6},{8,9},{9,8},{10,11... | collective-permute-start | bytes 786440 | tf_op jit(solution)/shard_map/ppermute | solution.py:275
  15.3 1.1 %turned_piece.1 = bf16[512,256]{1,0:T(8,128)(2,1)S(1)} custom-call(s32[1]{0:T(128)} %bitcast.k_ref.refs_0_, bf16[8,2,2,64,512]{4,3,2,1,0:T(8,128)(2,1)} %refs_1_.3), custom_call_target="tpu_custom_call" | custom-call | tf_op jit(solution)/shard_map/turned_piece/pallas_call | solution.py:226
  16.4 0.2 collective-permute-start
  16.6 0.1 copy.8.refs_6_
  16.7 5.3 %collective-permute-start.4 = (s32[8,2]{1,0:T(8,128)S(1)}, s32[8,2]{1,0:T(8,128)S(1)}, u32[]{:S(2)}, u32[]{:S(2)}) collective-permute-start(s32[8,2]{1,0:T(8,128)S(1)} %copy.8.refs_6_), channel_id=1, source_target_pairs={{0,1},{1,0},{2,3},{3,2},{4,5},{5,4},{6,7},{7,6},{8,9},{9,8},{10,11... | collective-permute-start | bytes 200 | tf_op jit(solution)/shard_map/ppermute | solution.py:276
  22.0 0.0 copy-done
  22.0 3.5 %own_partials.1.refs_1_ = bf16[4,4,2,256,128]{4,3,2,1,0:T(8,128)(2,1)S(1)} custom-call(s32[1]{0:T(128)} %bitcast.k_ref.refs_0_, bf16[8,2,2,64,512]{4,3,2,1,0:T(8,128)(2,1)} %refs_1_.3, bf16[512,512]{1,0:T(8,128)(2,1)S(1)} %copy-done), custom_call_target="tpu_custom_call" | custom-call | flops 536870912 | bytes 4194304 | tf_op jit(solution)/shard_map/own_partials/pallas_call | solution.py:93
  25.4 0.0 collective-permute-done.3.refs_2_
  25.5 0.9 %beam_step.3.refs_5_ = f32[4,256,128]{2,1,0:T(8,128)S(1)} custom-call(s32[1]{0:T(128)} %bitcast.k_ref.refs_0_, bf16[4,4,2,256,128]{4,3,2,1,0:T(8,128)(2,1)S(1)} %own_partials.1.refs_1_, bf16[8,2,16,512]{3,2,1,0:T(8,128)(2,1)S(1)} %collective-permute-done.3.refs_2_, bf16[512,512]{1,0:T(8,128)(2,1)S(1)} %copy-done, bf16[256,256]{1,0:T(8,128)(2,1)S(1)} %copy-done.1), custom_call_target="tpu_custom_call" | custom-call | flops 268435456 | bytes 2097152 | tf_op jit(solution)/shard_map/beam_step/pallas_call | solution.py:171
  26.3 0.0 collective-permute-done.2.refs_2_
  26.3 0.9 %beam_step.4.refs_5_ = f32[4,256,128]{2,1,0:T(8,128)S(1)} custom-call(s32[1]{0:T(128)} %bitcast.k_ref.refs_0_, bf16[4,4,2,256,128]{4,3,2,1,0:T(8,128)(2,1)S(1)} %own_partials.1.refs_1_, bf16[8,2,16,512]{3,2,1,0:T(8,128)(2,1)S(1)} %collective-permute-done.2.refs_2_, bf16[512,512]{1,0:T(8,128)(2,1)S(1)} %copy-done, ...), custom_call_target="tpu_custom_call", output_to_operand_aliasing={{}: (5, {})} | custom-call | flops 268435456 | bytes 2097152 | tf_op jit(solution)/shard_map/beam_step/pallas_call | solution.py:171
  27.2 1.7 %collective-permute-done.1.refs_2_ = bf16[8,2,16,512]{3,2,1,0:T(8,128)(2,1)S(1)} collective-permute-done((bf16[8,2,16,512]{3,2,1,0:T(8,128)(2,1)S(1)}, bf16[8,2,16,512]{3,2,1,0:T(8,128)(2,1)S(1)}, u32[]{:S(2)}, u32[]{:S(2)}) %collective-permute-start.1) | collective-permute-done | bytes 262176 | tf_op jit(solution)/shard_map/ppermute | solution.py:275
  28.9 0.9 %beam_step.5.refs_5_ = f32[4,256,128]{2,1,0:T(8,128)S(1)} custom-call(s32[1]{0:T(128)} %bitcast.k_ref.refs_0_, bf16[4,4,2,256,128]{4,3,2,1,0:T(8,128)(2,1)S(1)} %own_partials.1.refs_1_, bf16[8,2,16,512]{3,2,1,0:T(8,128)(2,1)S(1)} %collective-permute-done.1.refs_2_, bf16[512,512]{1,0:T(8,128)(2,1)S(1)} %copy-done, ...), custom_call_target="tpu_custom_call", output_to_operand_aliasing={{}: (5, {})} | custom-call | flops 268435456 | bytes 2097152 | tf_op jit(solution)/shard_map/beam_step/pallas_call | solution.py:171
  29.8 7.4 %collective-permute-done.4.refs_7_ = s32[8,2]{1,0:T(8,128)S(1)} collective-permute-done((s32[8,2]{1,0:T(8,128)S(1)}, s32[8,2]{1,0:T(8,128)S(1)}, u32[]{:S(2)}, u32[]{:S(2)}) %collective-permute-start.4) | collective-permute-done | bytes 96 | tf_op jit(solution)/shard_map/ppermute | solution.py:276
  37.3 0.0 collective-permute-done.refs_2_
  37.3 0.7 beam_step_last.1
  38.0 46.2 %all_to_all.5 = bf16[256,4,128]{2,1,0:T(4,128)(2,1)S(1)} all-to-all(bf16[256,4,128]{2,1,0:T(4,128)(2,1)S(1)} %bitcast.8), channel_id=1, replica_groups=mesh['chan'=128,'cyl'=2] {'chan','cyl'}, dimensions={0} | all-to-all | bytes 524288 | tf_op jit(solution)/shard_map/all_to_all | solution.py:284
  84.1 0.9 %place.1 = f32[4,256,128]{2,1,0:T(8,128)} custom-call(bf16[1024,128]{1,0:T(8,128)(2,1)S(1)} %bitcast.9), custom_call_target="tpu_custom_call" | custom-call | tf_op jit(solution)/shard_map/place/pallas_call | solution.py:252
  (3 shorter events, 0.0 us)
Async XLA Ops:
  1.0 15.6 %copy-start.2 = (s32[8,2]{0,1:T(2,128)S(1)}, s32[8,2]{0,1:T(2,128)}, u32[]{:S(2)}) copy-start(s32[8,2]{0,1:T(2,128)} %param.5) | copy-start | bytes 196
  1.0 21.0 %copy-start = (bf16[512,512]{1,0:T(8,128)(2,1)S(1)}, bf16[512,512]{1,0:T(8,128)(2,1)}, u32[]{:S(2)}) copy-start(bf16[512,512]{1,0:T(8,128)(2,1)} %constant.8.clone.t_ref.refs_3_) | copy-start | bytes 1572868
  1.0 24.5 %collective-permute-start.3 = (bf16[8,2,16,512]{3,2,1,0:T(8,128)(2,1)S(1)}, bf16[8,2,16,512]{3,2,1,0:T(8,128)(2,1)S(1)}, u32[]{:S(2)}, u32[]{:S(2)}) collective-permute-start(bf16[8,2,16,512]{3,2,1,0:T(8,128)(2,1)S(1)} %split.3), channel_id=1, source_target_pairs={{0,1},{1,0},{2,3},{3,2},{4,5},{5,4},{6,7},{7,6},{8,9},{9,8},{10,11... | collective-permute-start | bytes 786440 | tf_op jit(solution)/shard_map/ppermute | solution.py:275
  9.9 16.5 %collective-permute-start.2 = (bf16[8,2,16,512]{3,2,1,0:T(8,128)(2,1)S(1)}, bf16[8,2,16,512]{3,2,1,0:T(8,128)(2,1)S(1)}, u32[]{:S(2)}, u32[]{:S(2)}) collective-permute-start(bf16[8,2,16,512]{3,2,1,0:T(8,128)(2,1)S(1)} %get-tuple-element.8), channel_id=1, source_target_pairs={{0,1},{1,0},{2,3},{3,2},{4,5},{5,4},{6,7},{7,6},{8,9},{9,8},{10,11... | collective-permute-start | bytes 786440 | tf_op jit(solution)/shard_map/ppermute | solution.py:275
  10.0 18.9 %collective-permute-start.1 = (bf16[8,2,16,512]{3,2,1,0:T(8,128)(2,1)S(1)}, bf16[8,2,16,512]{3,2,1,0:T(8,128)(2,1)S(1)}, u32[]{:S(2)}, u32[]{:S(2)}) collective-permute-start(bf16[8,2,16,512]{3,2,1,0:T(8,128)(2,1)S(1)} %get-tuple-element.7), channel_id=1, source_target_pairs={{0,1},{1,0},{2,3},{3,2},{4,5},{5,4},{6,7},{7,6},{8,9},{9,8},{10,11... | collective-permute-start | bytes 786440 | tf_op jit(solution)/shard_map/ppermute | solution.py:275
  16.4 20.9 %collective-permute-start = (bf16[512,256]{1,0:T(8,128)(2,1)S(1)}, bf16[512,256]{1,0:T(8,128)(2,1)S(1)}, u32[]{:S(2)}, u32[]{:S(2)}) collective-permute-start(bf16[512,256]{1,0:T(8,128)(2,1)S(1)} %turned_piece.1), channel_id=1, source_target_pairs={{0,1},{1,0},{2,3},{3,2},{4,5},{5,4},{6,7},{7,6},{8,9},{9,8},{10,11... | collective-permute-start | bytes 786440 | tf_op jit(solution)/shard_map/ppermute | solution.py:275
  16.7 8.8 %copy-start.1 = (bf16[256,256]{1,0:T(8,128)(2,1)S(1)}, bf16[256,256]{1,0:T(8,128)(2,1)}, u32[]{:S(2)}) copy-start(bf16[256,256]{1,0:T(8,128)(2,1)} %constant.9.clone.refs_4_) | copy-start | bytes 393220
  16.7 20.6 %collective-permute-start.4 = (s32[8,2]{1,0:T(8,128)S(1)}, s32[8,2]{1,0:T(8,128)S(1)}, u32[]{:S(2)}, u32[]{:S(2)}) collective-permute-start(s32[8,2]{1,0:T(8,128)S(1)} %copy.8.refs_6_), channel_id=1, source_target_pairs={{0,1},{1,0},{2,3},{3,2},{4,5},{5,4},{6,7},{7,6},{8,9},{9,8},{10,11... | collective-permute-start | bytes 200 | tf_op jit(solution)/shard_map/ppermute | solution.py:276

commit v5 on v4

--- a/solution.py
+++ b/solution.py
@@ -51,7 +51,7 @@
 
 def ns_partials(x, t_ref, low, sign, turned=False):
     dims = (((1,), (0 if turned else 1,)), ((), ()))
-    half = FEEDS // 2
+    half = FEEDS if turned else FEEDS // 2
     real = lax.dot_general(t_ref[pl.ds(low * half, half), :], x, dims, preferred_element_type=jnp.float32)
     imag = lax.dot_general(t_ref[pl.ds(FEEDS + low * half, half), :], x, dims, preferred_element_type=jnp.float32)
     cut = lambda v: [v[:, :LANES], v[:, LANES:]]
@@ -125,8 +125,8 @@
     sign = (1 - 2 * k).astype(jnp.float32)
     x = recv_ref[...] if last else pair_rows(lambda cyl: recv_ref[:, cyl])
     half = FEEDS // 2
-    for low in range(2):
-        rows = pl.ds(low * half, half)
+    for low in range(1 if last else 2):
+        rows = slice(None) if last else pl.ds(low * half, half)
         for e, (other_r, other_i) in enumerate(ns_partials(x, t_ref, low, sign, last)):
             own_r, own_i = own_ref[0, e, 0, rows, :], own_ref[0, e, 1, rows, :]
             if e % 2 == 0:
@@ -140,7 +140,9 @@
             if not first:
                 power = acc_in[e, rows, :] + power
             if last:
-                stage_ref[pl.ds(2 * e + low, half, stride=8), :] = power * scale[e]
+                power = power * scale[e]
+                for bit in range(2):
+                    stage_ref[pl.ds(2 * e + bit, half, stride=8), :] = power[bit * half : (bit + 1) * half]
             else:
                 out_ref[e, rows, :] = power
     if last:

time: 85.2 us -> 85.1 us (level)
  no operation moved by 1% of the time
where the time goes in v5:
time: 85.1 us; the launch traced here: 84.9 us
  blocking collectives  46.2 us (54%)
  starting transfers between devices  18.8 us (22%)
  Pallas kernels  10.6 us (12%)
  waiting for transfers between devices  9.17 us (11%)
    all_to_all x1, blocking collectives, local(): lax.all_to_all(sent, ('chan', 'cyl'), split_axis=0, concat_axis=0, tiled=...  46.2 us
    ppermute x4, starting transfers between devices, local(): received = [lax.ppermute(piece, 'cyl', pair) for piece in pieces]  13.5 us
    ppermute x1, waiting for transfers between devices, local(): others = lax.ppermute(gain_exponents, 'cyl', pair)  7.45 us
    ppermute x1, starting transfers between devices, local(): others = lax.ppermute(gain_exponents, 'cyl', pair)  5.29 us
    pallas_call x1, Pallas kernels, own_partials(): pl.pallas_call(own_kernel, out_shape=jax.ShapeDtypeStruct(shape, jnp.bflo...  3.46 us
    pallas_call x4, Pallas kernels, step(): pl.pallas_call(lambda *refs: step_kernel(first, last, *refs), out_shape=o...  3.2 us
    pallas_call x2, Pallas kernels, split(): pl.pallas_call(lambda *refs: split_kernel(steps, *refs), out_shape=[piece...  2 us
    ppermute x4, waiting for transfers between devices, local(): received = [lax.ppermute(piece, 'cyl', pair) for piece in pieces]  1.72 us
  transfers between devices with their start and end apart: 5, of which 2 were waited for; matrix products, arithmetic and copies ran while one was open for 0% of the time, Pallas kernels for 10%

profile of v5, /device:TPU:1, one launch (start us, length us, event | category | flops | bytes accessed | tf_op | source)
XLA Modules:
  0.0 84.9 jit_solution(15322465574288883548)
XLA Ops:
  0.0 1.0 %split.3 = bf16[8,2,16,512]{3,2,1,0:T(8,128)(2,1)S(1)} custom-call(s32[1]{0:T(128)} %bitcast.k_ref.refs_0_, bf16[8,2,2,64,512]{4,3,2,1,0:T(8,128)(2,1)} %refs_1_.3), custom_call_target="tpu_custom_call" | custom-call | tf_op jit(solution)/shard_map/split/pallas_call | solution.py:207
  1.0 0.0 copy-start.2
  1.0 0.0 copy-start
  1.0 7.8 %collective-permute-start.3 = (bf16[8,2,16,512]{3,2,1,0:T(8,128)(2,1)S(1)}, bf16[8,2,16,512]{3,2,1,0:T(8,128)(2,1)S(1)}, u32[]{:S(2)}, u32[]{:S(2)}) collective-permute-start(bf16[8,2,16,512]{3,2,1,0:T(8,128)(2,1)S(1)} %split.3), channel_id=1, source_target_pairs={{0,1},{1,0},{2,3},{3,2},{4,5},{5,4},{6,7},{7,6},{8,9},{9,8},{10,11... | collective-permute-start | bytes 786440 | tf_op jit(solution)/shard_map/ppermute | solution.py:277
  8.8 1.0 %split.2 = (bf16[8,2,16,512]{3,2,1,0:T(8,128)(2,1)S(1)}, bf16[8,2,16,512]{3,2,1,0:T(8,128)(2,1)S(1)}) custom-call(s32[1]{0:T(128)} %bitcast.k_ref.refs_0_, bf16[8,2,2,64,512]{4,3,2,1,0:T(8,128)(2,1)} %refs_1_.3), custom_call_target="tpu_custom_call" | custom-call | tf_op jit(solution)/shard_map/split/pallas_call | solution.py:207
  9.9 0.2 collective-permute-start.2
  10.0 5.3 %collective-permute-start.1 = (bf16[8,2,16,512]{3,2,1,0:T(8,128)(2,1)S(1)}, bf16[8,2,16,512]{3,2,1,0:T(8,128)(2,1)S(1)}, u32[]{:S(2)}, u32[]{:S(2)}) collective-permute-start(bf16[8,2,16,512]{3,2,1,0:T(8,128)(2,1)S(1)} %get-tuple-element.7), channel_id=1, source_target_pairs={{0,1},{1,0},{2,3},{3,2},{4,5},{5,4},{6,7},{7,6},{8,9},{9,8},{10,11... | collective-permute-start | bytes 786440 | tf_op jit(solution)/shard_map/ppermute | solution.py:277
  15.3 1.1 %turned_piece.1 = bf16[512,256]{1,0:T(8,128)(2,1)S(1)} custom-call(s32[1]{0:T(128)} %bitcast.k_ref.refs_0_, bf16[8,2,2,64,512]{4,3,2,1,0:T(8,128)(2,1)} %refs_1_.3), custom_call_target="tpu_custom_call" | custom-call | tf_op jit(solution)/shard_map/turned_piece/pallas_call | solution.py:228
  16.4 0.2 collective-permute-start
  16.6 0.1 copy.8.refs_6_
  16.7 5.3 %collective-permute-start.4 = (s32[8,2]{1,0:T(8,128)S(1)}, s32[8,2]{1,0:T(8,128)S(1)}, u32[]{:S(2)}, u32[]{:S(2)}) collective-permute-start(s32[8,2]{1,0:T(8,128)S(1)} %copy.8.refs_6_), channel_id=1, source_target_pairs={{0,1},{1,0},{2,3},{3,2},{4,5},{5,4},{6,7},{7,6},{8,9},{9,8},{10,11... | collective-permute-start | bytes 200 | tf_op jit(solution)/shard_map/ppermute | solution.py:278
  22.0 0.0 copy-done
  22.0 3.5 %own_partials.1.refs_1_ = bf16[4,4,2,256,128]{4,3,2,1,0:T(8,128)(2,1)S(1)} custom-call(s32[1]{0:T(128)} %bitcast.k_ref.refs_0_, bf16[8,2,2,64,512]{4,3,2,1,0:T(8,128)(2,1)} %refs_1_.3, bf16[512,512]{1,0:T(8,128)(2,1)S(1)} %copy-done), custom_call_target="tpu_custom_call" | custom-call | flops 536870912 | bytes 4194304 | tf_op jit(solution)/shard_map/own_partials/pallas_call | solution.py:93
  25.4 0.0 collective-permute-done.3.refs_2_
  25.5 0.9 %beam_step.3.refs_5_ = f32[4,256,128]{2,1,0:T(8,128)S(1)} custom-call(s32[1]{0:T(128)} %bitcast.k_ref.refs_0_, bf16[4,4,2,256,128]{4,3,2,1,0:T(8,128)(2,1)S(1)} %own_partials.1.refs_1_, bf16[8,2,16,512]{3,2,1,0:T(8,128)(2,1)S(1)} %collective-permute-done.3.refs_2_, bf16[512,512]{1,0:T(8,128)(2,1)S(1)} %copy-done, bf16[256,256]{1,0:T(8,128)(2,1)S(1)} %copy-done.1), custom_call_target="tpu_custom_call" | custom-call | flops 268435456 | bytes 2097152 | tf_op jit(solution)/shard_map/beam_step/pallas_call | solution.py:173
  26.3 0.0 collective-permute-done.2.refs_2_
  26.3 0.9 %beam_step.4.refs_5_ = f32[4,256,128]{2,1,0:T(8,128)S(1)} custom-call(s32[1]{0:T(128)} %bitcast.k_ref.refs_0_, bf16[4,4,2,256,128]{4,3,2,1,0:T(8,128)(2,1)S(1)} %own_partials.1.refs_1_, bf16[8,2,16,512]{3,2,1,0:T(8,128)(2,1)S(1)} %collective-permute-done.2.refs_2_, bf16[512,512]{1,0:T(8,128)(2,1)S(1)} %copy-done, ...), custom_call_target="tpu_custom_call", output_to_operand_aliasing={{}: (5, {})} | custom-call | flops 268435456 | bytes 2097152 | tf_op jit(solution)/shard_map/beam_step/pallas_call | solution.py:173
  27.2 1.7 %collective-permute-done.1.refs_2_ = bf16[8,2,16,512]{3,2,1,0:T(8,128)(2,1)S(1)} collective-permute-done((bf16[8,2,16,512]{3,2,1,0:T(8,128)(2,1)S(1)}, bf16[8,2,16,512]{3,2,1,0:T(8,128)(2,1)S(1)}, u32[]{:S(2)}, u32[]{:S(2)}) %collective-permute-start.1) | collective-permute-done | bytes 262176 | tf_op jit(solution)/shard_map/ppermute | solution.py:277
  28.9 0.9 %beam_step.5.refs_5_ = f32[4,256,128]{2,1,0:T(8,128)S(1)} custom-call(s32[1]{0:T(128)} %bitcast.k_ref.refs_0_, bf16[4,4,2,256,128]{4,3,2,1,0:T(8,128)(2,1)S(1)} %own_partials.1.refs_1_, bf16[8,2,16,512]{3,2,1,0:T(8,128)(2,1)S(1)} %collective-permute-done.1.refs_2_, bf16[512,512]{1,0:T(8,128)(2,1)S(1)} %copy-done, ...), custom_call_target="tpu_custom_call", output_to_operand_aliasing={{}: (5, {})} | custom-call | flops 268435456 | bytes 2097152 | tf_op jit(solution)/shard_map/beam_step/pallas_call | solution.py:173
  29.8 7.4 %collective-permute-done.4.refs_7_ = s32[8,2]{1,0:T(8,128)S(1)} collective-permute-done((s32[8,2]{1,0:T(8,128)S(1)}, s32[8,2]{1,0:T(8,128)S(1)}, u32[]{:S(2)}, u32[]{:S(2)}) %collective-permute-start.4) | collective-permute-done | bytes 96 | tf_op jit(solution)/shard_map/ppermute | solution.py:278
  37.3 0.0 collective-permute-done.refs_2_
  37.3 0.6 beam_step_last.1
  37.9 46.2 %all_to_all.5 = bf16[256,4,128]{2,1,0:T(4,128)(2,1)S(1)} all-to-all(bf16[256,4,128]{2,1,0:T(4,128)(2,1)S(1)} %bitcast.8), channel_id=1, replica_groups=mesh['chan'=128,'cyl'=2] {'chan','cyl'}, dimensions={0} | all-to-all | bytes 524288 | tf_op jit(solution)/shard_map/all_to_all | solution.py:286
  84.0 0.9 %place.1 = f32[4,256,128]{2,1,0:T(8,128)} custom-call(bf16[1024,128]{1,0:T(8,128)(2,1)S(1)} %bitcast.9), custom_call_target="tpu_custom_call" | custom-call | tf_op jit(solution)/shard_map/place/pallas_call | solution.py:254
  (3 shorter events, 0.0 us)
Async XLA Ops:
  1.0 15.6 %copy-start.2 = (s32[8,2]{0,1:T(2,128)S(1)}, s32[8,2]{0,1:T(2,128)}, u32[]{:S(2)}) copy-start(s32[8,2]{0,1:T(2,128)} %param.5) | copy-start | bytes 196
  1.0 21.0 %copy-start = (bf16[512,512]{1,0:T(8,128)(2,1)S(1)}, bf16[512,512]{1,0:T(8,128)(2,1)}, u32[]{:S(2)}) copy-start(bf16[512,512]{1,0:T(8,128)(2,1)} %constant.8.clone.t_ref.refs_3_) | copy-start | bytes 1572868
  1.0 24.5 %collective-permute-start.3 = (bf16[8,2,16,512]{3,2,1,0:T(8,128)(2,1)S(1)}, bf16[8,2,16,512]{3,2,1,0:T(8,128)(2,1)S(1)}, u32[]{:S(2)}, u32[]{:S(2)}) collective-permute-start(bf16[8,2,16,512]{3,2,1,0:T(8,128)(2,1)S(1)} %split.3), channel_id=1, source_target_pairs={{0,1},{1,0},{2,3},{3,2},{4,5},{5,4},{6,7},{7,6},{8,9},{9,8},{10,11... | collective-permute-start | bytes 786440 | tf_op jit(solution)/shard_map/ppermute | solution.py:277
  9.9 16.5 %collective-permute-start.2 = (bf16[8,2,16,512]{3,2,1,0:T(8,128)(2,1)S(1)}, bf16[8,2,16,512]{3,2,1,0:T(8,128)(2,1)S(1)}, u32[]{:S(2)}, u32[]{:S(2)}) collective-permute-start(bf16[8,2,16,512]{3,2,1,0:T(8,128)(2,1)S(1)} %get-tuple-element.8), channel_id=1, source_target_pairs={{0,1},{1,0},{2,3},{3,2},{4,5},{5,4},{6,7},{7,6},{8,9},{9,8},{10,11... | collective-permute-start | bytes 786440 | tf_op jit(solution)/shard_map/ppermute | solution.py:277
  10.0 18.9 %collective-permute-start.1 = (bf16[8,2,16,512]{3,2,1,0:T(8,128)(2,1)S(1)}, bf16[8,2,16,512]{3,2,1,0:T(8,128)(2,1)S(1)}, u32[]{:S(2)}, u32[]{:S(2)}) collective-permute-start(bf16[8,2,16,512]{3,2,1,0:T(8,128)(2,1)S(1)} %get-tuple-element.7), channel_id=1, source_target_pairs={{0,1},{1,0},{2,3},{3,2},{4,5},{5,4},{6,7},{7,6},{8,9},{9,8},{10,11... | collective-permute-start | bytes 786440 | tf_op jit(solution)/shard_map/ppermute | solution.py:277
  16.4 20.9 %collective-permute-start = (bf16[512,256]{1,0:T(8,128)(2,1)S(1)}, bf16[512,256]{1,0:T(8,128)(2,1)S(1)}, u32[]{:S(2)}, u32[]{:S(2)}) collective-permute-start(bf16[512,256]{1,0:T(8,128)(2,1)S(1)} %turned_piece.1), channel_id=1, source_target_pairs={{0,1},{1,0},{2,3},{3,2},{4,5},{5,4},{6,7},{7,6},{8,9},{9,8},{10,11... | collective-permute-start | bytes 786440 | tf_op jit(solution)/shard_map/ppermute | solution.py:277
  16.7 8.8 %copy-start.1 = (bf16[256,256]{1,0:T(8,128)(2,1)S(1)}, bf16[256,256]{1,0:T(8,128)(2,1)}, u32[]{:S(2)}) copy-start(bf16[256,256]{1,0:T(8,128)(2,1)} %constant.9.clone.refs_4_) | copy-start | bytes 393220
  16.7 20.6 %collective-permute-start.4 = (s32[8,2]{1,0:T(8,128)S(1)}, s32[8,2]{1,0:T(8,128)S(1)}, u32[]{:S(2)}, u32[]{:S(2)}) collective-permute-start(s32[8,2]{1,0:T(8,128)S(1)} %copy.8.refs_6_), channel_id=1, source_target_pairs={{0,1},{1,0},{2,3},{3,2},{4,5},{5,4},{6,7},{7,6},{8,9},{9,8},{10,11... | collective-permute-start | bytes 200 | tf_op jit(solution)/shard_map/ppermute | solution.py:278

commit v6 on v5

--- a/solution.py
+++ b/solution.py
@@ -245,15 +245,23 @@
 
 
 def place_kernel(in_ref, out_ref, wide_ref):
-    wide_ref[...] = in_ref[...].astype(jnp.float32)
-    for row in range(4):
-        out_ref[row] = wide_ref[pl.ds(row, 256, stride=4), :]
+    first = 2 * pl.program_id(0)
+
+    @pl.when(first == 0)
+    def _():
+        wide_ref[...] = in_ref[...].astype(jnp.float32)
+
+    for row in range(2):
+        out_ref[row] = wide_ref[pl.ds(first + row, 256, stride=4), :]
 
 
 def place(arrived):
     return pl.pallas_call(
         place_kernel,
         out_shape=jax.ShapeDtypeStruct((4, 256, LANES), jnp.float32),
+        grid=(2,),
+        in_specs=[pl.BlockSpec((1024, LANES), lambda i: (0, 0))],
+        out_specs=pl.BlockSpec((2, 256, LANES), lambda i: (i, 0, 0)),
         scratch_shapes=[pltpu.VMEM((1024, LANES), jnp.float32)],
         compiler_params=pltpu.CompilerParams(vmem_limit_bytes=8 << 20),
         name="place",

time: 85.1 us -> 85.1 us (level)
  no operation moved by 1% of the time
where the time goes in v6:
time: 85.1 us; the launch traced here: 84.9 us
  blocking collectives  46.2 us (54%)
  starting transfers between devices  18.8 us (22%)
  Pallas kernels  10.6 us (12%)
  waiting for transfers between devices  9.17 us (11%)
    all_to_all x1, blocking collectives, local(): lax.all_to_all(sent, ('chan', 'cyl'), split_axis=0, concat_axis=0, tiled=...  46.2 us
    ppermute x4, starting transfers between devices, local(): received = [lax.ppermute(piece, 'cyl', pair) for piece in pieces]  13.5 us
    ppermute x1, waiting for transfers between devices, local(): others = lax.ppermute(gain_exponents, 'cyl', pair)  7.45 us
    ppermute x1, starting transfers between devices, local(): others = lax.ppermute(gain_exponents, 'cyl', pair)  5.29 us
    pallas_call x1, Pallas kernels, own_partials(): pl.pallas_call(own_kernel, out_shape=jax.ShapeDtypeStruct(shape, jnp.bflo...  3.46 us
    pallas_call x4, Pallas kernels, step(): pl.pallas_call(lambda *refs: step_kernel(first, last, *refs), out_shape=o...  3.2 us
    pallas_call x2, Pallas kernels, split(): pl.pallas_call(lambda *refs: split_kernel(steps, *refs), out_shape=[piece...  2 us
    ppermute x4, waiting for transfers between devices, local(): received = [lax.ppermute(piece, 'cyl', pair) for piece in pieces]  1.72 us
  transfers between devices with their start and end apart: 5, of which 2 were waited for; matrix products, arithmetic and copies ran while one was open for 0% of the time, Pallas kernels for 10%

profile of v6, /device:TPU:1, one launch (start us, length us, event | category | flops | bytes accessed | tf_op | source)
XLA Modules:
  0.0 84.9 jit_solution(6953103977749553913)
XLA Ops:
  0.0 1.0 %split.3 = bf16[8,2,16,512]{3,2,1,0:T(8,128)(2,1)S(1)} custom-call(s32[1]{0:T(128)} %bitcast.k_ref.refs_0_, bf16[8,2,2,64,512]{4,3,2,1,0:T(8,128)(2,1)} %refs_1_.3), custom_call_target="tpu_custom_call" | custom-call | tf_op jit(solution)/shard_map/split/pallas_call | solution.py:207
  1.0 0.0 copy-start.2
  1.0 0.0 copy-start
  1.0 7.8 %collective-permute-start.3 = (bf16[8,2,16,512]{3,2,1,0:T(8,128)(2,1)S(1)}, bf16[8,2,16,512]{3,2,1,0:T(8,128)(2,1)S(1)}, u32[]{:S(2)}, u32[]{:S(2)}) collective-permute-start(bf16[8,2,16,512]{3,2,1,0:T(8,128)(2,1)S(1)} %split.3), channel_id=1, source_target_pairs={{0,1},{1,0},{2,3},{3,2},{4,5},{5,4},{6,7},{7,6},{8,9},{9,8},{10,11... | collective-permute-start | bytes 786440 | tf_op jit(solution)/shard_map/ppermute | solution.py:285
  8.8 1.0 %split.2 = (bf16[8,2,16,512]{3,2,1,0:T(8,128)(2,1)S(1)}, bf16[8,2,16,512]{3,2,1,0:T(8,128)(2,1)S(1)}) custom-call(s32[1]{0:T(128)} %bitcast.k_ref.refs_0_, bf16[8,2,2,64,512]{4,3,2,1,0:T(8,128)(2,1)} %refs_1_.3), custom_call_target="tpu_custom_call" | custom-call | tf_op jit(solution)/shard_map/split/pallas_call | solution.py:207
  9.9 0.2 collective-permute-start.2
  10.0 5.3 %collective-permute-start.1 = (bf16[8,2,16,512]{3,2,1,0:T(8,128)(2,1)S(1)}, bf16[8,2,16,512]{3,2,1,0:T(8,128)(2,1)S(1)}, u32[]{:S(2)}, u32[]{:S(2)}) collective-permute-start(bf16[8,2,16,512]{3,2,1,0:T(8,128)(2,1)S(1)} %get-tuple-element.7), channel_id=1, source_target_pairs={{0,1},{1,0},{2,3},{3,2},{4,5},{5,4},{6,7},{7,6},{8,9},{9,8},{10,11... | collective-permute-start | bytes 786440 | tf_op jit(solution)/shard_map/ppermute | solution.py:285
  15.3 1.1 %turned_piece.1 = bf16[512,256]{1,0:T(8,128)(2,1)S(1)} custom-call(s32[1]{0:T(128)} %bitcast.k_ref.refs_0_, bf16[8,2,2,64,512]{4,3,2,1,0:T(8,128)(2,1)} %refs_1_.3), custom_call_target="tpu_custom_call" | custom-call | tf_op jit(solution)/shard_map/turned_piece/pallas_call | solution.py:228
  16.4 0.2 collective-permute-start
  16.6 0.1 copy.8.refs_6_
  16.7 5.3 %collective-permute-start.4 = (s32[8,2]{1,0:T(8,128)S(1)}, s32[8,2]{1,0:T(8,128)S(1)}, u32[]{:S(2)}, u32[]{:S(2)}) collective-permute-start(s32[8,2]{1,0:T(8,128)S(1)} %copy.8.refs_6_), channel_id=1, source_target_pairs={{0,1},{1,0},{2,3},{3,2},{4,5},{5,4},{6,7},{7,6},{8,9},{9,8},{10,11... | collective-permute-start | bytes 200 | tf_op jit(solution)/shard_map/ppermute | solution.py:286
  22.0 0.0 copy-done
  22.0 3.5 %own_partials.1.refs_1_ = bf16[4,4,2,256,128]{4,3,2,1,0:T(8,128)(2,1)S(1)} custom-call(s32[1]{0:T(128)} %bitcast.k_ref.refs_0_, bf16[8,2,2,64,512]{4,3,2,1,0:T(8,128)(2,1)} %refs_1_.3, bf16[512,512]{1,0:T(8,128)(2,1)S(1)} %copy-done), custom_call_target="tpu_custom_call" | custom-call | flops 536870912 | bytes 4194304 | tf_op jit(solution)/shard_map/own_partials/pallas_call | solution.py:93
  25.4 0.0 collective-permute-done.3.refs_2_
  25.5 0.9 %beam_step.3.refs_5_ = f32[4,256,128]{2,1,0:T(8,128)S(1)} custom-call(s32[1]{0:T(128)} %bitcast.k_ref.refs_0_, bf16[4,4,2,256,128]{4,3,2,1,0:T(8,128)(2,1)S(1)} %own_partials.1.refs_1_, bf16[8,2,16,512]{3,2,1,0:T(8,128)(2,1)S(1)} %collective-permute-done.3.refs_2_, bf16[512,512]{1,0:T(8,128)(2,1)S(1)} %copy-done, bf16[256,256]{1,0:T(8,128)(2,1)S(1)} %copy-done.1), custom_call_target="tpu_custom_call" | custom-call | flops 268435456 | bytes 2097152 | tf_op jit(solution)/shard_map/beam_step/pallas_call | solution.py:173
  26.3 0.0 collective-permute-done.2.refs_2_
  26.3 0.9 %beam_step.4.refs_5_ = f32[4,256,128]{2,1,0:T(8,128)S(1)} custom-call(s32[1]{0:T(128)} %bitcast.k_ref.refs_0_, bf16[4,4,2,256,128]{4,3,2,1,0:T(8,128)(2,1)S(1)} %own_partials.1.refs_1_, bf16[8,2,16,512]{3,2,1,0:T(8,128)(2,1)S(1)} %collective-permute-done.2.refs_2_, bf16[512,512]{1,0:T(8,128)(2,1)S(1)} %copy-done, ...), custom_call_target="tpu_custom_call", output_to_operand_aliasing={{}: (5, {})} | custom-call | flops 268435456 | bytes 2097152 | tf_op jit(solution)/shard_map/beam_step/pallas_call | solution.py:173
  27.2 1.7 %collective-permute-done.1.refs_2_ = bf16[8,2,16,512]{3,2,1,0:T(8,128)(2,1)S(1)} collective-permute-done((bf16[8,2,16,512]{3,2,1,0:T(8,128)(2,1)S(1)}, bf16[8,2,16,512]{3,2,1,0:T(8,128)(2,1)S(1)}, u32[]{:S(2)}, u32[]{:S(2)}) %collective-permute-start.1) | collective-permute-done | bytes 262176 | tf_op jit(solution)/shard_map/ppermute | solution.py:285
  28.9 0.9 %beam_step.5.refs_5_ = f32[4,256,128]{2,1,0:T(8,128)S(1)} custom-call(s32[1]{0:T(128)} %bitcast.k_ref.refs_0_, bf16[4,4,2,256,128]{4,3,2,1,0:T(8,128)(2,1)S(1)} %own_partials.1.refs_1_, bf16[8,2,16,512]{3,2,1,0:T(8,128)(2,1)S(1)} %collective-permute-done.1.refs_2_, bf16[512,512]{1,0:T(8,128)(2,1)S(1)} %copy-done, ...), custom_call_target="tpu_custom_call", output_to_operand_aliasing={{}: (5, {})} | custom-call | flops 268435456 | bytes 2097152 | tf_op jit(solution)/shard_map/beam_step/pallas_call | solution.py:173
  29.8 7.4 %collective-permute-done.4.refs_7_ = s32[8,2]{1,0:T(8,128)S(1)} collective-permute-done((s32[8,2]{1,0:T(8,128)S(1)}, s32[8,2]{1,0:T(8,128)S(1)}, u32[]{:S(2)}, u32[]{:S(2)}) %collective-permute-start.4) | collective-permute-done | bytes 96 | tf_op jit(solution)/shard_map/ppermute | solution.py:286
  37.3 0.0 collective-permute-done.refs_2_
  37.3 0.6 beam_step_last.1
  37.9 46.2 %all_to_all.5 = bf16[256,4,128]{2,1,0:T(4,128)(2,1)S(1)} all-to-all(bf16[256,4,128]{2,1,0:T(4,128)(2,1)S(1)} %bitcast.8), channel_id=1, replica_groups=mesh['chan'=128,'cyl'=2] {'chan','cyl'}, dimensions={0} | all-to-all | bytes 524288 | tf_op jit(solution)/shard_map/all_to_all | solution.py:294
  84.0 0.8 place.1
  (3 shorter events, 0.0 us)
Async XLA Ops:
  1.0 15.6 %copy-start.2 = (s32[8,2]{0,1:T(2,128)S(1)}, s32[8,2]{0,1:T(2,128)}, u32[]{:S(2)}) copy-start(s32[8,2]{0,1:T(2,128)} %param.5) | copy-start | bytes 196
  1.0 21.0 %copy-start = (bf16[512,512]{1,0:T(8,128)(2,1)S(1)}, bf16[512,512]{1,0:T(8,128)(2,1)}, u32[]{:S(2)}) copy-start(bf16[512,512]{1,0:T(8,128)(2,1)} %constant.8.clone.t_ref.refs_3_) | copy-start | bytes 1572868
  1.0 24.5 %collective-permute-start.3 = (bf16[8,2,16,512]{3,2,1,0:T(8,128)(2,1)S(1)}, bf16[8,2,16,512]{3,2,1,0:T(8,128)(2,1)S(1)}, u32[]{:S(2)}, u32[]{:S(2)}) collective-permute-start(bf16[8,2,16,512]{3,2,1,0:T(8,128)(2,1)S(1)} %split.3), channel_id=1, source_target_pairs={{0,1},{1,0},{2,3},{3,2},{4,5},{5,4},{6,7},{7,6},{8,9},{9,8},{10,11... | collective-permute-start | bytes 786440 | tf_op jit(solution)/shard_map/ppermute | solution.py:285
  9.9 16.5 %collective-permute-start.2 = (bf16[8,2,16,512]{3,2,1,0:T(8,128)(2,1)S(1)}, bf16[8,2,16,512]{3,2,1,0:T(8,128)(2,1)S(1)}, u32[]{:S(2)}, u32[]{:S(2)}) collective-permute-start(bf16[8,2,16,512]{3,2,1,0:T(8,128)(2,1)S(1)} %get-tuple-element.8), channel_id=1, source_target_pairs={{0,1},{1,0},{2,3},{3,2},{4,5},{5,4},{6,7},{7,6},{8,9},{9,8},{10,11... | collective-permute-start | bytes 786440 | tf_op jit(solution)/shard_map/ppermute | solution.py:285
  10.0 18.9 %collective-permute-start.1 = (bf16[8,2,16,512]{3,2,1,0:T(8,128)(2,1)S(1)}, bf16[8,2,16,512]{3,2,1,0:T(8,128)(2,1)S(1)}, u32[]{:S(2)}, u32[]{:S(2)}) collective-permute-start(bf16[8,2,16,512]{3,2,1,0:T(8,128)(2,1)S(1)} %get-tuple-element.7), channel_id=1, source_target_pairs={{0,1},{1,0},{2,3},{3,2},{4,5},{5,4},{6,7},{7,6},{8,9},{9,8},{10,11... | collective-permute-start | bytes 786440 | tf_op jit(solution)/shard_map/ppermute | solution.py:285
  16.4 20.9 %collective-permute-start = (bf16[512,256]{1,0:T(8,128)(2,1)S(1)}, bf16[512,256]{1,0:T(8,128)(2,1)S(1)}, u32[]{:S(2)}, u32[]{:S(2)}) collective-permute-start(bf16[512,256]{1,0:T(8,128)(2,1)S(1)} %turned_piece.1), channel_id=1, source_target_pairs={{0,1},{1,0},{2,3},{3,2},{4,5},{5,4},{6,7},{7,6},{8,9},{9,8},{10,11... | collective-permute-start | bytes 786440 | tf_op jit(solution)/shard_map/ppermute | solution.py:285
  16.7 8.8 %copy-start.1 = (bf16[256,256]{1,0:T(8,128)(2,1)S(1)}, bf16[256,256]{1,0:T(8,128)(2,1)}, u32[]{:S(2)}) copy-start(bf16[256,256]{1,0:T(8,128)(2,1)} %constant.9.clone.refs_4_) | copy-start | bytes 393220
  16.7 20.6 %collective-permute-start.4 = (s32[8,2]{1,0:T(8,128)S(1)}, s32[8,2]{1,0:T(8,128)S(1)}, u32[]{:S(2)}, u32[]{:S(2)}) collective-permute-start(s32[8,2]{1,0:T(8,128)S(1)} %copy.8.refs_6_), channel_id=1, source_target_pairs={{0,1},{1,0},{2,3},{3,2},{4,5},{5,4},{6,7},{7,6},{8,9},{9,8},{10,11... | collective-permute-start | bytes 200 | tf_op jit(solution)/shard_map/ppermute | solution.py:286

commit v7 on v5

--- a/solution.py
+++ b/solution.py
@@ -113,13 +113,13 @@
 
 def step_kernel(first, last, *refs):
     refs = list(refs)
-    k_ref, own_ref, recv_ref, t_ref, u_ref = refs[:5]
-    refs = refs[5:]
+    own_ref, recv_ref, t_ref, u_ref = refs[:4]
+    refs = refs[4:]
     acc_in = None if first else refs.pop(0)
     gain_refs = [refs.pop(0), refs.pop(0)] if last else None
     out_ref = refs.pop(0)
     stage_ref = refs.pop(0) if last else None
-    k = k_ref[0]
+    k = lax.axis_index("cyl")
     if last:
         scale = gain_rows(k, *gain_refs)
     sign = (1 - 2 * k).astype(jnp.float32)
@@ -149,18 +149,18 @@
         out_ref[...] = stage_ref[...].astype(jnp.bfloat16)
 
 
-def step(index, first, last, k, own, recv, table, up_table, acc, gains):
-    whole = lambda a: pl.BlockSpec(a.shape, lambda i, kk: (0,) * a.ndim)
+def step(index, first, last, own, recv, table, up_table, acc, gains):
+    whole = lambda a: pl.BlockSpec(a.shape, lambda i: (0,) * a.ndim)
     args = [own, recv, table, up_table]
     specs = [
-        pl.BlockSpec((1, *own.shape[1:]), lambda i, kk: (index, 0, 0, 0, 0)),
+        pl.BlockSpec((1, *own.shape[1:]), lambda i: (index, 0, 0, 0, 0)),
         whole(recv),
         whole(table),
         whole(up_table),
     ]
     aliases = {}
     if not first:
-        aliases = {} if last else {len(args) + 1: 0}
+        aliases = {} if last else {len(args): 0}
         args.append(acc)
         specs.append(whole(acc))
     if last:
@@ -173,18 +173,15 @@
     return pl.pallas_call(
         lambda *refs: step_kernel(first, last, *refs),
         out_shape=out,
-        grid_spec=pltpu.PrefetchScalarGridSpec(
-            num_scalar_prefetch=1,
-            grid=(1,),
-            in_specs=specs,
-            out_specs=whole(out),
-            scratch_shapes=[pltpu.VMEM((FEEDS * CYLS, LANES), jnp.float32)] if last else [],
-        ),
+        grid=(1,),
+        in_specs=specs,
+        out_specs=whole(out),
+        scratch_shapes=[pltpu.VMEM((FEEDS * CYLS, LANES), jnp.float32)] if last else [],
         input_output_aliases=aliases,
         cost_estimate=pl.CostEstimate(flops=flops, bytes_accessed=2 << 20, transcendentals=0),
         compiler_params=pltpu.CompilerParams(vmem_limit_bytes=8 << 20),
         name="beam_step_last" if last else "beam_step",
-    )(k, *args)
+    )(*args)
 
 
 def split_kernel(steps, k_ref, volts_ref, *refs):
@@ -281,7 +278,7 @@
     gains = (gain_exponents, others)
     for index in range(len(steps)):
         first, last = index == 0, index == len(steps) - 1
-        acc = step(index, first, last, which, own, received[index], table, up_table, acc, gains)
+        acc = step(index, first, last, own, received[index], table, up_table, acc, gains)
     sent = acc.reshape(256, 4, LANES)
     arrived = lax.all_to_all(sent, ("chan", "cyl"), split_axis=0, concat_axis=0, tiled=True)
     placed = place(arrived.reshape(1024, LANES))

time: 85.1 us -> 85.1 us (level)
  no operation moved by 1% of the time
where the time goes in v7:
time: 85.1 us; the launch traced here: 84.9 us
  blocking collectives  46.2 us (54%)
  starting transfers between devices  18.8 us (22%)
  Pallas kernels  10.6 us (12%)
  waiting for transfers between devices  9.19 us (11%)
    all_to_all x1, blocking collectives, local(): lax.all_to_all(sent, ('chan', 'cyl'), split_axis=0, concat_axis=0, tiled=...  46.2 us
    ppermute x4, starting transfers between devices, local(): received = [lax.ppermute(piece, 'cyl', pair) for piece in pieces]  13.5 us
    ppermute x1, waiting for transfers between devices, local(): others = lax.ppermute(gain_exponents, 'cyl', pair)  7.46 us
    ppermute x1, starting transfers between devices, local(): others = lax.ppermute(gain_exponents, 'cyl', pair)  5.29 us
    pallas_call x1, Pallas kernels, own_partials(): pl.pallas_call(own_kernel, out_shape=jax.ShapeDtypeStruct(shape, jnp.bflo...  3.46 us
    pallas_call x4, Pallas kernels, step(): pl.pallas_call(lambda *refs: step_kernel(first, last, *refs), out_shape=o...  3.17 us
    pallas_call x2, Pallas kernels, split(): pl.pallas_call(lambda *refs: split_kernel(steps, *refs), out_shape=[piece...  2 us
    ppermute x4, waiting for transfers between devices, local(): received = [lax.ppermute(piece, 'cyl', pair) for piece in pieces]  1.73 us
  transfers between devices with their start and end apart: 5, of which 2 were waited for; matrix products, arithmetic and copies ran while one was open for 0% of the time, Pallas kernels for 10%

profile of v7, /device:TPU:1, one launch (start us, length us, event | category | flops | bytes accessed | tf_op | source)
XLA Modules:
  0.0 84.9 jit_solution(12035914587149040938)
XLA Ops:
  0.0 1.0 %split.3 = bf16[8,2,16,512]{3,2,1,0:T(8,128)(2,1)S(1)} custom-call(s32[1]{0:T(128)} %bitcast.k_ref.refs_0_, bf16[8,2,2,64,512]{4,3,2,1,0:T(8,128)(2,1)} %refs_1_.3), custom_call_target="tpu_custom_call" | custom-call | tf_op jit(solution)/shard_map/split/pallas_call | solution.py:204
  1.0 0.0 copy-start.2
  1.0 0.0 copy-start
  1.0 7.8 %collective-permute-start.3 = (bf16[8,2,16,512]{3,2,1,0:T(8,128)(2,1)S(1)}, bf16[8,2,16,512]{3,2,1,0:T(8,128)(2,1)S(1)}, u32[]{:S(2)}, u32[]{:S(2)}) collective-permute-start(bf16[8,2,16,512]{3,2,1,0:T(8,128)(2,1)S(1)} %split.3), channel_id=1, source_target_pairs={{0,1},{1,0},{2,3},{3,2},{4,5},{5,4},{6,7},{7,6},{8,9},{9,8},{10,11... | collective-permute-start | bytes 786440 | tf_op jit(solution)/shard_map/ppermute | solution.py:274
  8.8 1.0 %split.2 = (bf16[8,2,16,512]{3,2,1,0:T(8,128)(2,1)S(1)}, bf16[8,2,16,512]{3,2,1,0:T(8,128)(2,1)S(1)}) custom-call(s32[1]{0:T(128)} %bitcast.k_ref.refs_0_, bf16[8,2,2,64,512]{4,3,2,1,0:T(8,128)(2,1)} %refs_1_.3), custom_call_target="tpu_custom_call" | custom-call | tf_op jit(solution)/shard_map/split/pallas_call | solution.py:204
  9.9 0.2 collective-permute-start.2
  10.0 5.3 %collective-permute-start.1 = (bf16[8,2,16,512]{3,2,1,0:T(8,128)(2,1)S(1)}, bf16[8,2,16,512]{3,2,1,0:T(8,128)(2,1)S(1)}, u32[]{:S(2)}, u32[]{:S(2)}) collective-permute-start(bf16[8,2,16,512]{3,2,1,0:T(8,128)(2,1)S(1)} %get-tuple-element.7), channel_id=1, source_target_pairs={{0,1},{1,0},{2,3},{3,2},{4,5},{5,4},{6,7},{7,6},{8,9},{9,8},{10,11... | collective-permute-start | bytes 786440 | tf_op jit(solution)/shard_map/ppermute | solution.py:274
  15.3 1.1 %turned_piece.1 = bf16[512,256]{1,0:T(8,128)(2,1)S(1)} custom-call(s32[1]{0:T(128)} %bitcast.k_ref.refs_0_, bf16[8,2,2,64,512]{4,3,2,1,0:T(8,128)(2,1)} %refs_1_.3), custom_call_target="tpu_custom_call" | custom-call | tf_op jit(solution)/shard_map/turned_piece/pallas_call | solution.py:225
  16.4 0.2 collective-permute-start
  16.6 0.1 copy.8.refs_5_
  16.7 5.3 %collective-permute-start.4 = (s32[8,2]{1,0:T(8,128)S(1)}, s32[8,2]{1,0:T(8,128)S(1)}, u32[]{:S(2)}, u32[]{:S(2)}) collective-permute-start(s32[8,2]{1,0:T(8,128)S(1)} %copy.8.refs_5_), channel_id=1, source_target_pairs={{0,1},{1,0},{2,3},{3,2},{4,5},{5,4},{6,7},{7,6},{8,9},{9,8},{10,11... | collective-permute-start | bytes 200 | tf_op jit(solution)/shard_map/ppermute | solution.py:275
  22.0 0.0 copy-done
  22.0 3.5 %own_partials.1.refs_0_ = bf16[4,4,2,256,128]{4,3,2,1,0:T(8,128)(2,1)S(1)} custom-call(s32[1]{0:T(128)} %bitcast.k_ref.refs_0_, bf16[8,2,2,64,512]{4,3,2,1,0:T(8,128)(2,1)} %refs_1_.3, bf16[512,512]{1,0:T(8,128)(2,1)S(1)} %copy-done), custom_call_target="tpu_custom_call" | custom-call | flops 536870912 | bytes 4194304 | tf_op jit(solution)/shard_map/own_partials/pallas_call | solution.py:93
  25.4 0.0 collective-permute-done.3.refs_1_
  25.5 0.8 beam_step.3.refs_4_
  26.3 0.0 collective-permute-done.2.refs_1_
  26.3 0.9 %beam_step.4.refs_4_ = f32[4,256,128]{2,1,0:T(8,128)S(1)} custom-call(bf16[4,4,2,256,128]{4,3,2,1,0:T(8,128)(2,1)S(1)} %own_partials.1.refs_0_, bf16[8,2,16,512]{3,2,1,0:T(8,128)(2,1)S(1)} %collective-permute-done.2.refs_1_, bf16[512,512]{1,0:T(8,128)(2,1)S(1)} %copy-done, bf16[256,256]{1,0:T(8,128)(2,1)S(1)} %copy-done.1, ...), custom_call_target="tpu_custom_call", output_to_operand_aliasing={{}: (4, {})} | custom-call | flops 268435456 | bytes 2097152 | tf_op jit(solution)/shard_map/beam_step/pallas_call | solution.py:173
  27.2 1.7 %collective-permute-done.1.refs_1_ = bf16[8,2,16,512]{3,2,1,0:T(8,128)(2,1)S(1)} collective-permute-done((bf16[8,2,16,512]{3,2,1,0:T(8,128)(2,1)S(1)}, bf16[8,2,16,512]{3,2,1,0:T(8,128)(2,1)S(1)}, u32[]{:S(2)}, u32[]{:S(2)}) %collective-permute-start.1) | collective-permute-done | bytes 262176 | tf_op jit(solution)/shard_map/ppermute | solution.py:274
  28.9 0.9 %beam_step.5.refs_4_ = f32[4,256,128]{2,1,0:T(8,128)S(1)} custom-call(bf16[4,4,2,256,128]{4,3,2,1,0:T(8,128)(2,1)S(1)} %own_partials.1.refs_0_, bf16[8,2,16,512]{3,2,1,0:T(8,128)(2,1)S(1)} %collective-permute-done.1.refs_1_, bf16[512,512]{1,0:T(8,128)(2,1)S(1)} %copy-done, bf16[256,256]{1,0:T(8,128)(2,1)S(1)} %copy-done.1, ...), custom_call_target="tpu_custom_call", output_to_operand_aliasing={{}: (4, {})} | custom-call | flops 268435456 | bytes 2097152 | tf_op jit(solution)/shard_map/beam_step/pallas_call | solution.py:173
  29.8 7.5 %collective-permute-done.4.refs_6_ = s32[8,2]{1,0:T(8,128)S(1)} collective-permute-done((s32[8,2]{1,0:T(8,128)S(1)}, s32[8,2]{1,0:T(8,128)S(1)}, u32[]{:S(2)}, u32[]{:S(2)}) %collective-permute-start.4) | collective-permute-done | bytes 96 | tf_op jit(solution)/shard_map/ppermute | solution.py:275
  37.3 0.0 collective-permute-done.refs_1_
  37.3 0.6 beam_step_last.1
  37.9 46.2 %all_to_all.5 = bf16[256,4,128]{2,1,0:T(4,128)(2,1)S(1)} all-to-all(bf16[256,4,128]{2,1,0:T(4,128)(2,1)S(1)} %bitcast.9), channel_id=1, replica_groups=mesh['chan'=128,'cyl'=2] {'chan','cyl'}, dimensions={0} | all-to-all | bytes 524288 | tf_op jit(solution)/shard_map/all_to_all | solution.py:283
  84.0 0.9 %place.1 = f32[4,256,128]{2,1,0:T(8,128)} custom-call(bf16[1024,128]{1,0:T(8,128)(2,1)S(1)} %bitcast.8), custom_call_target="tpu_custom_call" | custom-call | tf_op jit(solution)/shard_map/place/pallas_call | solution.py:251
  (3 shorter events, 0.0 us)
Async XLA Ops:
  1.0 15.6 %copy-start.2 = (s32[8,2]{0,1:T(2,128)S(1)}, s32[8,2]{0,1:T(2,128)}, u32[]{:S(2)}) copy-start(s32[8,2]{0,1:T(2,128)} %param.5) | copy-start | bytes 196
  1.0 21.0 %copy-start = (bf16[512,512]{1,0:T(8,128)(2,1)S(1)}, bf16[512,512]{1,0:T(8,128)(2,1)}, u32[]{:S(2)}) copy-start(bf16[512,512]{1,0:T(8,128)(2,1)} %constant.8.clone.t_ref.refs_2_) | copy-start | bytes 1572868
  1.0 24.5 %collective-permute-start.3 = (bf16[8,2,16,512]{3,2,1,0:T(8,128)(2,1)S(1)}, bf16[8,2,16,512]{3,2,1,0:T(8,128)(2,1)S(1)}, u32[]{:S(2)}, u32[]{:S(2)}) collective-permute-start(bf16[8,2,16,512]{3,2,1,0:T(8,128)(2,1)S(1)} %split.3), channel_id=1, source_target_pairs={{0,1},{1,0},{2,3},{3,2},{4,5},{5,4},{6,7},{7,6},{8,9},{9,8},{10,11... | collective-permute-start | bytes 786440 | tf_op jit(solution)/shard_map/ppermute | solution.py:274
  9.9 16.4 %collective-permute-start.2 = (bf16[8,2,16,512]{3,2,1,0:T(8,128)(2,1)S(1)}, bf16[8,2,16,512]{3,2,1,0:T(8,128)(2,1)S(1)}, u32[]{:S(2)}, u32[]{:S(2)}) collective-permute-start(bf16[8,2,16,512]{3,2,1,0:T(8,128)(2,1)S(1)} %get-tuple-element.8), channel_id=1, source_target_pairs={{0,1},{1,0},{2,3},{3,2},{4,5},{5,4},{6,7},{7,6},{8,9},{9,8},{10,11... | collective-permute-start | bytes 786440 | tf_op jit(solution)/shard_map/ppermute | solution.py:274
  10.0 18.9 %collective-permute-start.1 = (bf16[8,2,16,512]{3,2,1,0:T(8,128)(2,1)S(1)}, bf16[8,2,16,512]{3,2,1,0:T(8,128)(2,1)S(1)}, u32[]{:S(2)}, u32[]{:S(2)}) collective-permute-start(bf16[8,2,16,512]{3,2,1,0:T(8,128)(2,1)S(1)} %get-tuple-element.7), channel_id=1, source_target_pairs={{0,1},{1,0},{2,3},{3,2},{4,5},{5,4},{6,7},{7,6},{8,9},{9,8},{10,11... | collective-permute-start | bytes 786440 | tf_op jit(solution)/shard_map/ppermute | solution.py:274
  16.4 20.9 %collective-permute-start = (bf16[512,256]{1,0:T(8,128)(2,1)S(1)}, bf16[512,256]{1,0:T(8,128)(2,1)S(1)}, u32[]{:S(2)}, u32[]{:S(2)}) collective-permute-start(bf16[512,256]{1,0:T(8,128)(2,1)S(1)} %turned_piece.1), channel_id=1, source_target_pairs={{0,1},{1,0},{2,3},{3,2},{4,5},{5,4},{6,7},{7,6},{8,9},{9,8},{10,11... | collective-permute-start | bytes 786440 | tf_op jit(solution)/shard_map/ppermute | solution.py:274
  16.7 8.8 %copy-start.1 = (bf16[256,256]{1,0:T(8,128)(2,1)S(1)}, bf16[256,256]{1,0:T(8,128)(2,1)}, u32[]{:S(2)}) copy-start(bf16[256,256]{1,0:T(8,128)(2,1)} %constant.9.clone.refs_3_) | copy-start | bytes 393220
  16.7 20.6 %collective-permute-start.4 = (s32[8,2]{1,0:T(8,128)S(1)}, s32[8,2]{1,0:T(8,128)S(1)}, u32[]{:S(2)}, u32[]{:S(2)}) collective-permute-start(s32[8,2]{1,0:T(8,128)S(1)} %copy.8.refs_5_), channel_id=1, source_target_pairs={{0,1},{1,0},{2,3},{3,2},{4,5},{5,4},{6,7},{7,6},{8,9},{9,8},{10,11... | collective-permute-start | bytes 200 | tf_op jit(solution)/shard_map/ppermute | solution.py:275
